TPU v7x, 128 devices: a whole 4x4x4 slice. The times are simulated.
128 devices in a mesh: ctx: 16 (over y_lo, x, core), exp: 8 (over y_hi, z).
Axes of the slice: x: 4, y: 4 (y_hi: 2, y_lo: 2; y = y_hi * 2 + y_lo), z: 4, core: 2. Of those that a mesh axis runs over, the one named last changes fastest.
Arguments:
- queries: bfloat16 [2048, 3072], P('ctx', 'exp'), may hold values from -8 to 8
- keys: bfloat16 [2048, 1024], P('ctx', 'exp'), may hold values from -8 to 8
- values: bfloat16 [2048, 1024], P('ctx', 'exp'), may hold values from -6 to 6
- norm_gain: float32 [3072], replicated, may hold values from 0.1 to 1.9
- routes: int32 [2048, 2], P(('ctx', 'exp')), may hold values from 0 to 7, all different within a row; in each aligned block of 16 rows (0 to 15, 16 to 31, ...) at most 6 rows name the same one
- route_scores: float32 [2048, 2], P(('ctx', 'exp')), may hold values from -8 to 8
- cotangent: bfloat16 [2048, 3072], P(('ctx', 'exp')), may hold values from -6 to 6
- w_gate: bfloat16 [8, 3072, 8192], P('exp', None, 'ctx'), may hold values from -0.109375 to 0.109375
- w_up: bfloat16 [8, 3072, 8192], P('exp', None, 'ctx'), may hold values from -0.109375 to 0.109375
- w_down: bfloat16 [8, 8192, 3072], P('exp', 'ctx'), may hold values from -0.0625 to 0.0625
Outputs:
- mixed: bfloat16 [2048, 3072], P(('ctx', 'exp'))
- grad_input: bfloat16 [2048, 3072], P(('ctx', 'exp'))
- grad_gate: bfloat16 [8, 3072, 8192], P('exp', None, 'ctx')
- grad_up: bfloat16 [8, 3072, 8192], P('exp', None, 'ctx')
- grad_down: bfloat16 [8, 8192, 3072], P('exp', 'ctx')
Inputs may be any that keep to these rules, and one draw needn't show every extreme that they name: `routes`: each row names two different experts. Within each aligned block of 16 rows (the rows of one device) no expert is named by more than 6 rows, a bound that some block reaches.
All inputs are finite; a program needn't handle non-finite values.
Results may differ from a plain program's by a relative error of at most 0.018.
Values may be sent and summed in bfloat16 or wider, within the bound.
A program may use at most 128 MiB of HBM per device.

v0:
```python
import jax
import jax.numpy as jnp
from jax import lax
from jax.sharding import PartitionSpec as P

norm_eps = 1e-05
masked_value = -1e30


def shifted(block, axis, distance):
    devices = range(lax.axis_size(axis))
    route = [(i - distance, i) for i in devices if i - distance in devices]
    return lax.ppermute(block, axis, route)


def heads_first(query_local, group, head):
    count = query_local.shape[0]
    return query_local.reshape(count, group, head).transpose(1, 0, 2).reshape(group * count, head)


def attend_piece(state, query_flat, query_pos, piece, start, head):
    running_max, running_sum, accum = state
    key_part = piece[:, :head]
    value_part = piece[:, head:].astype(jnp.float32)
    scores = lax.dot_general(
        query_flat, key_part, (((1,), (1,)), ((), ())), preferred_element_type=jnp.float32
    ) * head ** (-0.5)
    key_pos = start + jnp.arange(piece.shape[0], dtype=jnp.int32)
    allowed = key_pos[None, :] <= query_pos[:, None]
    scores = jnp.where(allowed, scores, masked_value)
    new_max = jnp.maximum(running_max, jnp.max(scores, axis=1))
    weights = jnp.where(allowed, jnp.exp(scores - new_max[:, None]), 0.0)
    factor = jnp.exp(running_max - new_max)
    new_sum = running_sum * factor + jnp.sum(weights, axis=1)
    product = jnp.dot(
        weights, value_part, precision=lax.Precision.HIGHEST, preferred_element_type=jnp.float32
    )
    new_accum = accum * factor[:, None] + product
    return (new_max, new_sum, new_accum)


def local(queries, keys, values, norm_gain, routes, route_scores, cotangent, w_gate, w_up, w_down):
    n_ctx = lax.axis_size("ctx")
    n_exp = lax.axis_size("exp")
    head = keys.shape[1]
    group = queries.shape[1] // head
    tok_ctx = queries.shape[0]
    ctx_index = lax.axis_index("ctx")
    query_flat = heads_first(queries, group, head)
    query_pos = ctx_index * tok_ctx + jnp.tile(jnp.arange(tok_ctx, dtype=jnp.int32), group)
    key_values = jnp.concatenate([keys, values], axis=1)
    query_rows = query_flat.shape[0]
    initial = (
        jnp.full((query_rows,), masked_value, jnp.float32),
        jnp.zeros((query_rows,), jnp.float32),
        jnp.zeros((query_rows, head), jnp.float32),
    )
    first = attend_piece(initial, query_flat, query_pos, key_values, ctx_index * tok_ctx, head)

    def cycle_step(step, carry):
        state, current = carry
        current = shifted(current, "ctx", 1)
        source = (ctx_index - step) % n_ctx
        state = attend_piece(state, query_flat, query_pos, current, source * tok_ctx, head)
        return (state, current)

    state, _ = lax.fori_loop(1, n_ctx, cycle_step, (first, key_values))
    running_max, running_sum, accum = state
    attended = accum / running_sum[:, None]
    attended = (
        attended.reshape(group, tok_ctx, head)
        .transpose(1, 0, 2)
        .reshape(tok_ctx, group * head)
        .astype(jnp.bfloat16)
    )
    features = lax.all_to_all(attended, "exp", split_axis=0, concat_axis=1, tiled=True)
    feats = features.astype(jnp.float32)
    inv_rms = lax.rsqrt(jnp.mean(feats * feats, axis=1) + norm_eps)
    normed = (feats * inv_rms[:, None] * norm_gain[None, :]).astype(jnp.bfloat16)
    tok_dev = normed.shape[0]
    width = normed.shape[1]
    capacity = 3 * tok_dev // n_exp
    slots = n_exp * capacity
    flat_routes = routes.reshape(-1)
    onehot = (flat_routes[:, None] == jnp.arange(n_exp, dtype=jnp.int32)[None, :]).astype(jnp.int32)
    ranks = jnp.sum((jnp.cumsum(onehot, axis=0) - onehot) * onehot, axis=1)
    target = flat_routes * capacity + ranks
    placed = (jnp.arange(slots, dtype=jnp.int32)[:, None] == target[None, :]).astype(jnp.float32)
    place_tokens = placed.reshape(slots, tok_dev, 2).sum(axis=2)
    probs = jax.nn.softmax(route_scores, axis=1)
    mixing = (placed * probs.reshape(-1)[None, :]).reshape(slots, tok_dev, 2).sum(axis=2)
    send = jnp.dot(
        place_tokens.astype(jnp.bfloat16), normed, preferred_element_type=jnp.float32
    ).astype(jnp.bfloat16)
    arrived = lax.all_to_all(
        send.reshape(n_exp, capacity, width), "exp", split_axis=0, concat_axis=0, tiled=True
    ).reshape(slots, width)
    expert_in = lax.all_gather(arrived, "ctx", axis=0, tiled=True)
    gate_w = w_gate[0]
    up_w = w_up[0]
    down_w = w_down[0]
    gate_pre = jnp.dot(expert_in, gate_w, preferred_element_type=jnp.float32)
    up_pre = jnp.dot(expert_in, up_w, preferred_element_type=jnp.float32)
    hidden = (jax.nn.silu(gate_pre) * up_pre).astype(jnp.bfloat16)
    expert_out = lax.psum_scatter(
        jnp.dot(hidden, down_w, preferred_element_type=jnp.float32).astype(jnp.bfloat16),
        "ctx",
        scatter_dimension=0,
        tiled=True,
    )
    returned = lax.all_to_all(
        expert_out.reshape(n_exp, capacity, width), "exp", split_axis=0, concat_axis=0, tiled=True
    ).reshape(slots, width)
    mixed = lax.dot_general(
        mixing,
        returned.astype(jnp.float32),
        (((0,), (0,)), ((), ())),
        precision=lax.Precision.HIGHEST,
    ).astype(jnp.bfloat16)
    grad_slots = jnp.dot(
        mixing, cotangent.astype(jnp.float32), precision=lax.Precision.HIGHEST
    ).astype(jnp.bfloat16)
    grad_arrived = lax.all_to_all(
        grad_slots.reshape(n_exp, capacity, width), "exp", split_axis=0, concat_axis=0, tiled=True
    ).reshape(slots, width)
    grad_out, rows_in = (
        lax.all_gather(grad_arrived, "ctx", axis=0, tiled=True),
        lax.all_gather(arrived, "ctx", axis=0, tiled=True),
    )
    grad_hidden = lax.dot_general(
        grad_out, down_w, (((1,), (1,)), ((), ())), preferred_element_type=jnp.float32
    )
    grad_down = lax.dot_general(
        hidden, grad_out, (((0,), (0,)), ((), ())), preferred_element_type=jnp.float32
    ).astype(jnp.bfloat16)
    sig = jax.nn.sigmoid(gate_pre)
    grad_up_pre = (grad_hidden * (gate_pre * sig)).astype(jnp.bfloat16)
    grad_gate_pre = (grad_hidden * up_pre * sig * (1.0 + gate_pre * (1.0 - sig))).astype(
        jnp.bfloat16
    )
    grad_gate = lax.dot_general(
        rows_in, grad_gate_pre, (((0,), (0,)), ((), ())), preferred_element_type=jnp.float32
    ).astype(jnp.bfloat16)
    grad_upw = lax.dot_general(
        rows_in, grad_up_pre, (((0,), (0,)), ((), ())), preferred_element_type=jnp.float32
    ).astype(jnp.bfloat16)
    term = lax.dot_general(
        grad_gate_pre, gate_w, (((1,), (1,)), ((), ())), preferred_element_type=jnp.float32
    )
    grad_summed = lax.psum_scatter(
        (
            term
            + lax.dot_general(
                grad_up_pre, up_w, (((1,), (1,)), ((), ())), preferred_element_type=jnp.float32
            )
        ).astype(jnp.bfloat16),
        "ctx",
        scatter_dimension=0,
        tiled=True,
    )
    grad_back = lax.all_to_all(
        grad_summed.reshape(n_exp, capacity, width), "exp", split_axis=0, concat_axis=0, tiled=True
    ).reshape(slots, width)
    grad_normed = lax.dot_general(
        place_tokens,
        grad_back.astype(jnp.float32),
        (((0,), (0,)), ((), ())),
        precision=lax.Precision.HIGHEST,
    )
    weighted = grad_normed * norm_gain[None, :]
    inner = jnp.mean(weighted * feats, axis=1)
    grad_input = (inv_rms[:, None] * weighted - feats * (inv_rms**3 * inner)[:, None]).astype(
        jnp.bfloat16
    )
    return (mixed, grad_input, grad_gate[None], grad_upw[None], grad_down[None])


def solution(mesh):
    placed = (
        P("ctx", "exp"),
        P("ctx", "exp"),
        P("ctx", "exp"),
        P(),
        P(("ctx", "exp"), None),
        P(("ctx", "exp"), None),
        P(("ctx", "exp"), None),
        P("exp", None, "ctx"),
        P("exp", None, "ctx"),
        P("exp", "ctx", None),
    )
    return jax.shard_map(
        local,
        mesh=mesh,
        in_specs=placed,
        out_specs=(
            P(("ctx", "exp"), None),
            P(("ctx", "exp"), None),
            P("exp", None, "ctx"),
            P("exp", None, "ctx"),
            P("exp", "ctx", None),
        ),
        check_vma=False,
    )
```

profile of v0, /device:TPU:8, one launch (start us, length us, event | category | flops | bytes accessed | tf_op | source)
XLA Modules:
  0.0 439.5 jit_solution(11982174086630426389)
XLA Ops:
  7.2 1.2 copy.45
  8.5 1.4 pad_maximum_fusion
  11.0 1.2 convolution_add_fusion.1
  12.2 140.4 %while.22 = (s32[]{:T(128)}, f32[384]{0:T(512)S(1)}, f32[384]{0:T(512)S(1)}, f32[384,128]{1,0:T(8,128)S(1)}, bf16[128,256]{1,0:T(8,128)(2,1)}, /*index=5*/s32[]{...) while((s32[]{:T(128)}, f32[384]{0:T(512)S(1)}, ...), condition=%wide.region_11.12_spmd.clone, body=%wide.region_8.11_spmd.clone.sunk | while | flops 88720656 | bytes 1575218 | solution.py:67
  12.2 1.9 collective-permute-start
  14.2 5.9 %collective-permute-done = bf16[128,256]{1,0:T(8,128)(2,1)S(1)} collective-permute-done((bf16[128,256]{1,0:T(8,128)(2,1)}, bf16[128,256]{1,0:T(8,128)(2,1)S(1)}, u32[]{:S(2)}, u32[]{:S(2)}) %collective-permute-start) | collective-permute-done | bytes 65568 | tf_op jit(solution)/shard_map/while/body/eval_jaxpr/ppermute | solution.py:13
  21.6 1.9 collective-permute-start
  23.6 5.9 %collective-permute-done = bf16[128,256]{1,0:T(8,128)(2,1)S(1)} collective-permute-done((bf16[128,256]{1,0:T(8,128)(2,1)}, bf16[128,256]{1,0:T(8,128)(2,1)S(1)}, u32[]{:S(2)}, u32[]{:S(2)}) %collective-permute-start) | collective-permute-done | bytes 65568 | tf_op jit(solution)/shard_map/while/body/eval_jaxpr/ppermute | solution.py:13
  31.0 1.9 collective-permute-start
  32.9 5.9 %collective-permute-done = bf16[128,256]{1,0:T(8,128)(2,1)S(1)} collective-permute-done((bf16[128,256]{1,0:T(8,128)(2,1)}, bf16[128,256]{1,0:T(8,128)(2,1)S(1)}, u32[]{:S(2)}, u32[]{:S(2)}) %collective-permute-start) | collective-permute-done | bytes 65568 | tf_op jit(solution)/shard_map/while/body/eval_jaxpr/ppermute | solution.py:13
  40.3 1.9 collective-permute-start
  42.3 5.9 %collective-permute-done = bf16[128,256]{1,0:T(8,128)(2,1)S(1)} collective-permute-done((bf16[128,256]{1,0:T(8,128)(2,1)}, bf16[128,256]{1,0:T(8,128)(2,1)S(1)}, u32[]{:S(2)}, u32[]{:S(2)}) %collective-permute-start) | collective-permute-done | bytes 65568 | tf_op jit(solution)/shard_map/while/body/eval_jaxpr/ppermute | solution.py:13
  49.7 1.9 collective-permute-start
  51.6 5.9 %collective-permute-done = bf16[128,256]{1,0:T(8,128)(2,1)S(1)} collective-permute-done((bf16[128,256]{1,0:T(8,128)(2,1)}, bf16[128,256]{1,0:T(8,128)(2,1)S(1)}, u32[]{:S(2)}, u32[]{:S(2)}) %collective-permute-start) | collective-permute-done | bytes 65568 | tf_op jit(solution)/shard_map/while/body/eval_jaxpr/ppermute | solution.py:13
  59.0 1.9 collective-permute-start
  61.0 5.9 %collective-permute-done = bf16[128,256]{1,0:T(8,128)(2,1)S(1)} collective-permute-done((bf16[128,256]{1,0:T(8,128)(2,1)}, bf16[128,256]{1,0:T(8,128)(2,1)S(1)}, u32[]{:S(2)}, u32[]{:S(2)}) %collective-permute-start) | collective-permute-done | bytes 65568 | tf_op jit(solution)/shard_map/while/body/eval_jaxpr/ppermute | solution.py:13
  68.4 1.9 collective-permute-start
  70.3 5.9 %collective-permute-done = bf16[128,256]{1,0:T(8,128)(2,1)S(1)} collective-permute-done((bf16[128,256]{1,0:T(8,128)(2,1)}, bf16[128,256]{1,0:T(8,128)(2,1)S(1)}, u32[]{:S(2)}, u32[]{:S(2)}) %collective-permute-start) | collective-permute-done | bytes 65568 | tf_op jit(solution)/shard_map/while/body/eval_jaxpr/ppermute | solution.py:13
  77.7 1.9 collective-permute-start
  79.7 5.9 %collective-permute-done = bf16[128,256]{1,0:T(8,128)(2,1)S(1)} collective-permute-done((bf16[128,256]{1,0:T(8,128)(2,1)}, bf16[128,256]{1,0:T(8,128)(2,1)S(1)}, u32[]{:S(2)}, u32[]{:S(2)}) %collective-permute-start) | collective-permute-done | bytes 65568 | tf_op jit(solution)/shard_map/while/body/eval_jaxpr/ppermute | solution.py:13
  87.1 1.9 collective-permute-start
  89.0 5.9 %collective-permute-done = bf16[128,256]{1,0:T(8,128)(2,1)S(1)} collective-permute-done((bf16[128,256]{1,0:T(8,128)(2,1)}, bf16[128,256]{1,0:T(8,128)(2,1)S(1)}, u32[]{:S(2)}, u32[]{:S(2)}) %collective-permute-start) | collective-permute-done | bytes 65568 | tf_op jit(solution)/shard_map/while/body/eval_jaxpr/ppermute | solution.py:13
  96.4 1.9 collective-permute-start
  98.4 5.9 %collective-permute-done = bf16[128,256]{1,0:T(8,128)(2,1)S(1)} collective-permute-done((bf16[128,256]{1,0:T(8,128)(2,1)}, bf16[128,256]{1,0:T(8,128)(2,1)S(1)}, u32[]{:S(2)}, u32[]{:S(2)}) %collective-permute-start) | collective-permute-done | bytes 65568 | tf_op jit(solution)/shard_map/while/body/eval_jaxpr/ppermute | solution.py:13
  105.8 1.9 collective-permute-start
  107.7 5.9 %collective-permute-done = bf16[128,256]{1,0:T(8,128)(2,1)S(1)} collective-permute-done((bf16[128,256]{1,0:T(8,128)(2,1)}, bf16[128,256]{1,0:T(8,128)(2,1)S(1)}, u32[]{:S(2)}, u32[]{:S(2)}) %collective-permute-start) | collective-permute-done | bytes 65568 | tf_op jit(solution)/shard_map/while/body/eval_jaxpr/ppermute | solution.py:13
  115.1 1.9 collective-permute-start
  117.1 5.9 %collective-permute-done = bf16[128,256]{1,0:T(8,128)(2,1)S(1)} collective-permute-done((bf16[128,256]{1,0:T(8,128)(2,1)}, bf16[128,256]{1,0:T(8,128)(2,1)S(1)}, u32[]{:S(2)}, u32[]{:S(2)}) %collective-permute-start) | collective-permute-done | bytes 65568 | tf_op jit(solution)/shard_map/while/body/eval_jaxpr/ppermute | solution.py:13
  124.5 1.9 collective-permute-start
  126.4 5.9 %collective-permute-done = bf16[128,256]{1,0:T(8,128)(2,1)S(1)} collective-permute-done((bf16[128,256]{1,0:T(8,128)(2,1)}, bf16[128,256]{1,0:T(8,128)(2,1)S(1)}, u32[]{:S(2)}, u32[]{:S(2)}) %collective-permute-start) | collective-permute-done | bytes 65568 | tf_op jit(solution)/shard_map/while/body/eval_jaxpr/ppermute | solution.py:13
  133.8 1.9 collective-permute-start
  135.8 5.9 %collective-permute-done = bf16[128,256]{1,0:T(8,128)(2,1)S(1)} collective-permute-done((bf16[128,256]{1,0:T(8,128)(2,1)}, bf16[128,256]{1,0:T(8,128)(2,1)S(1)}, u32[]{:S(2)}, u32[]{:S(2)}) %collective-permute-start) | collective-permute-done | bytes 65568 | tf_op jit(solution)/shard_map/while/body/eval_jaxpr/ppermute | solution.py:13
  143.2 1.9 collective-permute-start
  145.1 6.0 %collective-permute-done = bf16[128,256]{1,0:T(8,128)(2,1)S(1)} collective-permute-done((bf16[128,256]{1,0:T(8,128)(2,1)}, bf16[128,256]{1,0:T(8,128)(2,1)S(1)}, u32[]{:S(2)}, u32[]{:S(2)}) %collective-permute-start) | collective-permute-done | bytes 65568 | tf_op jit(solution)/shard_map/while/body/eval_jaxpr/ppermute | solution.py:13
  153.6 7.1 %all-to-all-start = ((bf16[8,16,384]{2,1,0:T(8,128)(2,1)}), bf16[8,16,384]{2,1,0:T(8,128)(2,1)S(1)}, u32[]{:S(2)}, u32[]{:S(2)}) async-start(bf16[8,16,384]{2,1,0:T(8,128)(2,1)} %convert_element_type.88), calls=%async_computation | async-start | bytes 196608 | tf_op jit(solution)/shard_map/all_to_all | solution.py:76
  161.6 7.1 %all-to-all-done = bf16[8,16,384]{2,1,0:T(8,128)(2,1)S(1)} async-done(((bf16[8,16,384]{2,1,0:T(8,128)(2,1)}), bf16[8,16,384]{2,1,0:T(8,128)(2,1)S(1)}, u32[]{:S(2)}, u32[]{:S(2)}) %all-to-all-start) | async-done | bytes 98336 | tf_op jit(solution)/shard_map/all_to_all | solution.py:76
  169.8 1.8 reshape.128
  171.6 13.6 %all_to_all.30 = bf16[8,6,3072]{2,1,0:T(8,128)(2,1)} all-to-all(bf16[8,6,3072]{2,1,0:T(8,128)(2,1)} %reshape.128), channel_id=1, replica_groups=mesh['ctx'=16,'exp'=8] {'exp'}, dimensions={0} | all-to-all | bytes 589824 | tf_op jit(solution)/shard_map/all_to_all | solution.py:95
  185.2 1.8 reshape.129
  187.1 1.2 convolution_convert_fusion.4
  188.3 1.8 reshape.132
  190.1 16.9 %all_to_all.31 = bf16[8,6,3072]{2,1,0:T(8,128)(2,1)} all-to-all(bf16[8,6,3072]{2,1,0:T(8,128)(2,1)} %reshape.132), channel_id=1, replica_groups=mesh['ctx'=16,'exp'=8] {'exp'}, dimensions={0} | all-to-all | bytes 589824 | tf_op jit(solution)/shard_map/all_to_all | solution.py:123
  207.0 1.8 reshape.133
  208.9 12.0 %all-gather.3.cloned.1.call-done = bf16[768,3072]{1,0:T(8,128)(2,1)} async-done(((bf16[48,3072]{1,0:T(8,128)(2,1)}), bf16[768,3072]{1,0:T(8,128)(2,1)}) %all-gather.3.cloned.1.call-update) | async-done | bytes 4718608 | tf_op jit(solution)/shard_map/all_gather | solution.py:98
  220.9 7.2 %fusion.18 = f32[768,512]{1,0:T(8,128)} fusion(bf16[768,3072]{1,0:T(8,128)(2,1)} %all-gather.3.cloned.1.call-done, bf16[1,3072,512]{2,1,0:T(8,128)(2,1)} %param.20), kind=kOutput, calls=%fused_computation.33 | convolution fusion | flops 2415919104 | bytes 9437184 | tf_op jit(solution)/shard_map/dot_general | solution.py:103
  228.1 3.7 fusion.22
  231.8 30.2 %all-gather.5.cloned.1.call-done = bf16[768,3072]{1,0:T(8,128)(2,1)} async-done(((bf16[48,3072]{1,0:T(8,128)(2,1)}), bf16[768,3072]{1,0:T(8,128)(2,1)}) %all-gather.5.cloned.1.call-update) | async-done | bytes 4718608 | tf_op jit(solution)/shard_map/all_gather | solution.py:127
  262.0 7.0 %multiply_convert_fusion = (bf16[768,512]{1,0:T(8,128)(2,1)}, bf16[768,512]{1,0:T(8,128)(2,1)}, bf16[768,512]{1,0:T(8,128)(2,1)S(1)}) fusion(f32[768,512]{1,0:T(8,128)} %fusion.22, f32[768,512]{1,0:T(8,128)} %fusion.18, bf16[768,3072]{1,0:T(8,128)(2,1)} %all-gather.5.cloned.1.call-done, bf16[1,512,3072]{2,1,0:T(8,128)(2,1)S(1)} %copy-done), kind=kOutput, calls=%fused_computation.39 | convolution fusion | flops 2421817344 | bytes 13369344 | tf_op jit(solution)/shard_map/dot_general | solution.py:130
  269.9 4.2 convolution_convert_fusion
  274.4 4.9 %fusion.20 = f32[768,3072]{1,0:T(8,128)S(1)} fusion(bf16[768,512]{1,0:T(8,128)(2,1)} %get-tuple-element.249, bf16[1,3072,512]{2,1,0:T(8,128)(2,1)} %param.19), kind=kOutput, calls=%fused_computation.35 | convolution fusion | flops 2415919104 | bytes 13369344 | tf_op jit(solution)/shard_map/dot_general | solution.py:147
  279.3 4.4 %add_convert_fusion = bf16[768,3072]{1,0:T(8,128)(2,1)} fusion(f32[768,3072]{1,0:T(8,128)S(1)} %fusion.20, bf16[768,512]{1,0:T(8,128)(2,1)S(1)} %copy-done.2, bf16[1,3072,512]{2,1,0:T(8,128)(2,1)S(1)} %copy-done.1), kind=kOutput, calls=%fused_computation.17 | convolution fusion | flops 2420637696 | bytes 18087936 | tf_op jit(solution)/shard_map/dot_general | solution.py:153
  283.8 6.9 %fusion.13 = bf16[1,512,3072]{2,1,0:T(8,128)(2,1)} fusion(bf16[768,512]{1,0:T(8,128)(2,1)} %copy-done.9, bf16[768,3072]{1,0:T(8,128)(2,1)} %all-gather.5.cloned.1.call-done), kind=kOutput, calls=%fused_computation.24 | convolution fusion | flops 2417491968 | bytes 8650752 | tf_op jit(solution)/shard_map/dot_general | solution.py:133
  290.7 50.8 %reduce-scatter.3.cloned.1.call-done = bf16[48,3072]{1,0:T(8,128)(2,1)} async-done(((bf16[768,3072]{1,0:T(8,128)(2,1)}), bf16[48,3072]{1,0:T(8,128)(2,1)}) %reduce-scatter.3.cloned.1.call-update) | async-done | bytes 294928 | tf_op jit(solution)/shard_map/reduce_scatter | solution.py:105
  341.5 1.8 reshape.130
  343.3 6.3 %all-to-all-start.2 = ((bf16[8,6,3072]{2,1,0:T(8,128)(2,1)}), bf16[8,6,3072]{2,1,0:T(8,128)(2,1)}, u32[]{:S(2)}, u32[]{:S(2)}) async-start(bf16[8,6,3072]{2,1,0:T(8,128)(2,1)} %reshape.130), calls=%async_computation.3 | async-start | bytes 786432 | tf_op jit(solution)/shard_map/all_to_all | solution.py:111
  349.7 6.9 %fusion.12 = bf16[1,3072,512]{2,1,0:T(8,128)(2,1)} fusion(bf16[768,3072]{1,0:T(8,128)(2,1)} %all-gather.3.cloned.1.call-done, bf16[768,512]{1,0:T(8,128)(2,1)} %get-tuple-element.248), kind=kOutput, calls=%fused_computation.23 | convolution fusion | flops 2417491968 | bytes 8650752 | tf_op jit(solution)/shard_map/dot_general | solution.py:144
  356.6 53.8 %reduce-scatter.5.cloned.1.call-done = bf16[48,3072]{1,0:T(8,128)(2,1)} async-done(((bf16[768,3072]{1,0:T(8,128)(2,1)}), bf16[48,3072]{1,0:T(8,128)(2,1)}) %reduce-scatter.5.cloned.1.call-update) | async-done | bytes 294928 | tf_op jit(solution)/shard_map/reduce_scatter | solution.py:150
  410.3 1.8 reshape.134
  412.1 6.4 %all-to-all-start.4 = ((bf16[8,6,3072]{2,1,0:T(8,128)(2,1)}), bf16[8,6,3072]{2,1,0:T(8,128)(2,1)}, u32[]{:S(2)}, u32[]{:S(2)}) async-start(bf16[8,6,3072]{2,1,0:T(8,128)(2,1)} %reshape.134), calls=%async_computation.6 | async-start | bytes 786432 | tf_op jit(solution)/shard_map/all_to_all | solution.py:161
  418.6 6.9 %fusion.11 = bf16[1,3072,512]{2,1,0:T(8,128)(2,1)} fusion(bf16[768,3072]{1,0:T(8,128)(2,1)} %all-gather.3.cloned.1.call-done, bf16[768,512]{1,0:T(8,128)(2,1)} %get-tuple-element.249), kind=kOutput, calls=%fused_computation.22 | convolution fusion | flops 2417491968 | bytes 8650752 | tf_op jit(solution)/shard_map/dot_general | solution.py:141
  425.4 1.8 reshape.131
  427.3 1.9 convolution_convert_fusion.6
  429.1 1.8 reshape.135
  430.9 1.3 multiply_reduce_fusion
  (194 shorter events, 27.5 us)
Async XLA Ops:
  7.2 254.8 %copy-start = (bf16[1,512,3072]{2,1,0:T(8,128)(2,1)S(1)}, bf16[1,512,3072]{2,1,0:T(8,128)(2,1)}, u32[]{:S(2)}) copy-start(bf16[1,512,3072]{2,1,0:T(8,128)(2,1)} %param.21) | copy-start | bytes 9437188
  12.2 148.5 %copy-start.5 = (f32[16,2]{0,1:T(2,128)S(1)}, f32[16,2]{0,1:T(2,128)}, u32[]{:S(2)}) copy-start(f32[16,2]{0,1:T(2,128)} %param.17) | copy-start | bytes 388
  12.2 148.6 %copy-start.6 = (s32[16,2]{0,1:T(2,128)S(1)}, s32[16,2]{0,1:T(2,128)}, u32[]{:S(2)}) copy-start(s32[16,2]{0,1:T(2,128)} %param.16) | copy-start | bytes 388
  12.2 156.6 %copy-start.4 = (f32[3072]{0:T(1024)S(1)}, f32[3072]{0:T(1024)}, u32[]{:S(2)}) copy-start(f32[3072]{0:T(1024)} %param.15) | copy-start | bytes 36868
  12.2 7.9 %collective-permute-start = (bf16[128,256]{1,0:T(8,128)(2,1)}, bf16[128,256]{1,0:T(8,128)(2,1)S(1)}, u32[]{:S(2)}, u32[]{:S(2)}) collective-permute-start(bf16[128,256]{1,0:T(8,128)(2,1)} %get-tuple-element.331), channel_id=1, source_target_pairs={{0,8},{8,16},{16,24},{24,32},{32,40},{40,48},{48,56},{56,64},{64,7... | collective-permute-start | bytes 196616 | tf_op jit(solution)/shard_map/while/body/eval_jaxpr/ppermute | solution.py:13
  21.6 7.9 %collective-permute-start = (bf16[128,256]{1,0:T(8,128)(2,1)}, bf16[128,256]{1,0:T(8,128)(2,1)S(1)}, u32[]{:S(2)}, u32[]{:S(2)}) collective-permute-start(bf16[128,256]{1,0:T(8,128)(2,1)} %get-tuple-element.331), channel_id=1, source_target_pairs={{0,8},{8,16},{16,24},{24,32},{32,40},{40,48},{48,56},{56,64},{64,7... | collective-permute-start | bytes 196616 | tf_op jit(solution)/shard_map/while/body/eval_jaxpr/ppermute | solution.py:13
  31.0 7.9 %collective-permute-start = (bf16[128,256]{1,0:T(8,128)(2,1)}, bf16[128,256]{1,0:T(8,128)(2,1)S(1)}, u32[]{:S(2)}, u32[]{:S(2)}) collective-permute-start(bf16[128,256]{1,0:T(8,128)(2,1)} %get-tuple-element.331), channel_id=1, source_target_pairs={{0,8},{8,16},{16,24},{24,32},{32,40},{40,48},{48,56},{56,64},{64,7... | collective-permute-start | bytes 196616 | tf_op jit(solution)/shard_map/while/body/eval_jaxpr/ppermute | solution.py:13
  40.3 7.9 %collective-permute-start = (bf16[128,256]{1,0:T(8,128)(2,1)}, bf16[128,256]{1,0:T(8,128)(2,1)S(1)}, u32[]{:S(2)}, u32[]{:S(2)}) collective-permute-start(bf16[128,256]{1,0:T(8,128)(2,1)} %get-tuple-element.331), channel_id=1, source_target_pairs={{0,8},{8,16},{16,24},{24,32},{32,40},{40,48},{48,56},{56,64},{64,7... | collective-permute-start | bytes 196616 | tf_op jit(solution)/shard_map/while/body/eval_jaxpr/ppermute | solution.py:13
  49.7 7.9 %collective-permute-start = (bf16[128,256]{1,0:T(8,128)(2,1)}, bf16[128,256]{1,0:T(8,128)(2,1)S(1)}, u32[]{:S(2)}, u32[]{:S(2)}) collective-permute-start(bf16[128,256]{1,0:T(8,128)(2,1)} %get-tuple-element.331), channel_id=1, source_target_pairs={{0,8},{8,16},{16,24},{24,32},{32,40},{40,48},{48,56},{56,64},{64,7... | collective-permute-start | bytes 196616 | tf_op jit(solution)/shard_map/while/body/eval_jaxpr/ppermute | solution.py:13
  59.0 7.9 %collective-permute-start = (bf16[128,256]{1,0:T(8,128)(2,1)}, bf16[128,256]{1,0:T(8,128)(2,1)S(1)}, u32[]{:S(2)}, u32[]{:S(2)}) collective-permute-start(bf16[128,256]{1,0:T(8,128)(2,1)} %get-tuple-element.331), channel_id=1, source_target_pairs={{0,8},{8,16},{16,24},{24,32},{32,40},{40,48},{48,56},{56,64},{64,7... | collective-permute-start | bytes 196616 | tf_op jit(solution)/shard_map/while/body/eval_jaxpr/ppermute | solution.py:13
  68.4 7.9 %collective-permute-start = (bf16[128,256]{1,0:T(8,128)(2,1)}, bf16[128,256]{1,0:T(8,128)(2,1)S(1)}, u32[]{:S(2)}, u32[]{:S(2)}) collective-permute-start(bf16[128,256]{1,0:T(8,128)(2,1)} %get-tuple-element.331), channel_id=1, source_target_pairs={{0,8},{8,16},{16,24},{24,32},{32,40},{40,48},{48,56},{56,64},{64,7... | collective-permute-start | bytes 196616 | tf_op jit(solution)/shard_map/while/body/eval_jaxpr/ppermute | solution.py:13
  77.7 7.9 %collective-permute-start = (bf16[128,256]{1,0:T(8,128)(2,1)}, bf16[128,256]{1,0:T(8,128)(2,1)S(1)}, u32[]{:S(2)}, u32[]{:S(2)}) collective-permute-start(bf16[128,256]{1,0:T(8,128)(2,1)} %get-tuple-element.331), channel_id=1, source_target_pairs={{0,8},{8,16},{16,24},{24,32},{32,40},{40,48},{48,56},{56,64},{64,7... | collective-permute-start | bytes 196616 | tf_op jit(solution)/shard_map/while/body/eval_jaxpr/ppermute | solution.py:13
  87.1 7.9 %collective-permute-start = (bf16[128,256]{1,0:T(8,128)(2,1)}, bf16[128,256]{1,0:T(8,128)(2,1)S(1)}, u32[]{:S(2)}, u32[]{:S(2)}) collective-permute-start(bf16[128,256]{1,0:T(8,128)(2,1)} %get-tuple-element.331), channel_id=1, source_target_pairs={{0,8},{8,16},{16,24},{24,32},{32,40},{40,48},{48,56},{56,64},{64,7... | collective-permute-start | bytes 196616 | tf_op jit(solution)/shard_map/while/body/eval_jaxpr/ppermute | solution.py:13
  96.4 7.9 %collective-permute-start = (bf16[128,256]{1,0:T(8,128)(2,1)}, bf16[128,256]{1,0:T(8,128)(2,1)S(1)}, u32[]{:S(2)}, u32[]{:S(2)}) collective-permute-start(bf16[128,256]{1,0:T(8,128)(2,1)} %get-tuple-element.331), channel_id=1, source_target_pairs={{0,8},{8,16},{16,24},{24,32},{32,40},{40,48},{48,56},{56,64},{64,7... | collective-permute-start | bytes 196616 | tf_op jit(solution)/shard_map/while/body/eval_jaxpr/ppermute | solution.py:13
  105.8 7.9 %collective-permute-start = (bf16[128,256]{1,0:T(8,128)(2,1)}, bf16[128,256]{1,0:T(8,128)(2,1)S(1)}, u32[]{:S(2)}, u32[]{:S(2)}) collective-permute-start(bf16[128,256]{1,0:T(8,128)(2,1)} %get-tuple-element.331), channel_id=1, source_target_pairs={{0,8},{8,16},{16,24},{24,32},{32,40},{40,48},{48,56},{56,64},{64,7... | collective-permute-start | bytes 196616 | tf_op jit(solution)/shard_map/while/body/eval_jaxpr/ppermute | solution.py:13
  115.1 7.9 %collective-permute-start = (bf16[128,256]{1,0:T(8,128)(2,1)}, bf16[128,256]{1,0:T(8,128)(2,1)S(1)}, u32[]{:S(2)}, u32[]{:S(2)}) collective-permute-start(bf16[128,256]{1,0:T(8,128)(2,1)} %get-tuple-element.331), channel_id=1, source_target_pairs={{0,8},{8,16},{16,24},{24,32},{32,40},{40,48},{48,56},{56,64},{64,7... | collective-permute-start | bytes 196616 | tf_op jit(solution)/shard_map/while/body/eval_jaxpr/ppermute | solution.py:13
  124.5 7.9 %collective-permute-start = (bf16[128,256]{1,0:T(8,128)(2,1)}, bf16[128,256]{1,0:T(8,128)(2,1)S(1)}, u32[]{:S(2)}, u32[]{:S(2)}) collective-permute-start(bf16[128,256]{1,0:T(8,128)(2,1)} %get-tuple-element.331), channel_id=1, source_target_pairs={{0,8},{8,16},{16,24},{24,32},{32,40},{40,48},{48,56},{56,64},{64,7... | collective-permute-start | bytes 196616 | tf_op jit(solution)/shard_map/while/body/eval_jaxpr/ppermute | solution.py:13
  133.8 7.9 %collective-permute-start = (bf16[128,256]{1,0:T(8,128)(2,1)}, bf16[128,256]{1,0:T(8,128)(2,1)S(1)}, u32[]{:S(2)}, u32[]{:S(2)}) collective-permute-start(bf16[128,256]{1,0:T(8,128)(2,1)} %get-tuple-element.331), channel_id=1, source_target_pairs={{0,8},{8,16},{16,24},{24,32},{32,40},{40,48},{48,56},{56,64},{64,7... | collective-permute-start | bytes 196616 | tf_op jit(solution)/shard_map/while/body/eval_jaxpr/ppermute | solution.py:13
  143.2 8.0 %collective-permute-start = (bf16[128,256]{1,0:T(8,128)(2,1)}, bf16[128,256]{1,0:T(8,128)(2,1)S(1)}, u32[]{:S(2)}, u32[]{:S(2)}) collective-permute-start(bf16[128,256]{1,0:T(8,128)(2,1)} %get-tuple-element.331), channel_id=1, source_target_pairs={{0,8},{8,16},{16,24},{24,32},{32,40},{40,48},{48,56},{56,64},{64,7... | collective-permute-start | bytes 196616 | tf_op jit(solution)/shard_map/while/body/eval_jaxpr/ppermute | solution.py:13
  152.6 34.5 %copy-start.3 = (bf16[16,3072]{1,0:T(8,128)(2,1)S(1)}, bf16[16,3072]{1,0:T(8,128)(2,1)}, u32[]{:S(2)}) copy-start(bf16[16,3072]{1,0:T(8,128)(2,1)} %param.18) | copy-start | bytes 294916
  153.6 15.1 %all-to-all-start = ((bf16[8,16,384]{2,1,0:T(8,128)(2,1)}), bf16[8,16,384]{2,1,0:T(8,128)(2,1)S(1)}, u32[]{:S(2)}, u32[]{:S(2)}) async-start(bf16[8,16,384]{2,1,0:T(8,128)(2,1)} %convert_element_type.88), calls=%async_computation | async-start | bytes 196608 | tf_op jit(solution)/shard_map/all_to_all | solution.py:76
  160.7 60.2 %all-gather.3.cloned.1.call-start = ((), (), s32[]{:S(2)}) async-start(), calls=%async_computation.7 | async-start | bytes 5013504 | tf_op jit(solution)/shard_map/all_gather | solution.py:98
  187.1 74.9 %all-gather.5.cloned.1.call-start = ((), (), s32[]{:S(2)}) async-start(), calls=%async_computation.9 | async-start | bytes 5013504 | tf_op jit(solution)/shard_map/all_gather | solution.py:127
  208.9 132.7 %reduce-scatter.3.cloned.1.call-start = ((), (), s32[]{:S(2)}) async-start(), calls=%async_computation.8 | async-start | bytes 5013504 | tf_op jit(solution)/shard_map/reduce_scatter | solution.py:105
  220.9 7.2 %copy-start.7 = (bf16[768,3072]{1,0:T(8,128)(2,1)S(1)}, bf16[768,3072]{1,0:T(8,128)(2,1)}, u32[]{:S(2)}) copy-start(bf16[768,3072]{1,0:T(8,128)(2,1)} %all-gather.3.cloned.1.call-done) | copy-start | bytes 14155780
  220.9 7.2 %copy-start.8 = (bf16[1,3072,512]{2,1,0:T(8,128)(2,1)S(1)}, bf16[1,3072,512]{2,1,0:T(8,128)(2,1)}, u32[]{:S(2)}) copy-start(bf16[1,3072,512]{2,1,0:T(8,128)(2,1)} %param.19) | copy-start | bytes 9437188
  269.0 0.9 copy-start.9
  274.1 136.2 %reduce-scatter.5.cloned.1.call-start = ((), (), s32[]{:S(2)}) async-start(), calls=%async_computation.10 | async-start | bytes 5013504 | tf_op jit(solution)/shard_map/reduce_scatter | solution.py:150
  274.4 4.9 %copy-start.1 = (bf16[1,3072,512]{2,1,0:T(8,128)(2,1)S(1)}, bf16[1,3072,512]{2,1,0:T(8,128)(2,1)}, u32[]{:S(2)}) copy-start(bf16[1,3072,512]{2,1,0:T(8,128)(2,1)} %param.20) | copy-start | bytes 9437188
  274.4 4.9 %copy-start.2 = (bf16[768,512]{1,0:T(8,128)(2,1)S(1)}, bf16[768,512]{1,0:T(8,128)(2,1)}, u32[]{:S(2)}) copy-start(bf16[768,512]{1,0:T(8,128)(2,1)} %get-tuple-element.248) | copy-start | bytes 2359300
  343.3 68.8 %all-to-all-start.2 = ((bf16[8,6,3072]{2,1,0:T(8,128)(2,1)}), bf16[8,6,3072]{2,1,0:T(8,128)(2,1)}, u32[]{:S(2)}, u32[]{:S(2)}) async-start(bf16[8,6,3072]{2,1,0:T(8,128)(2,1)} %reshape.130), calls=%async_computation.3 | async-start | bytes 786432 | tf_op jit(solution)/shard_map/all_to_all | solution.py:111
  412.1 17.0 %all-to-all-start.4 = ((bf16[8,6,3072]{2,1,0:T(8,128)(2,1)}), bf16[8,6,3072]{2,1,0:T(8,128)(2,1)}, u32[]{:S(2)}, u32[]{:S(2)}) async-start(bf16[8,6,3072]{2,1,0:T(8,128)(2,1)} %reshape.134), calls=%async_computation.6 | async-start | bytes 786432 | tf_op jit(solution)/shard_map/all_to_all | solution.py:161
Sparse Core Ops, SparseCore 0:
  187.2 33.6 all-gather.2
  223.1 38.7 all-gather.4
  274.2 67.2 reduce-scatter.2
  343.8 66.4 reduce-scatter.4
where the time goes:
time: 443 us; the launch traced here: 440 us
  waiting for transfers between devices  243 us (55%)
  matrix products  69.4 us (16%)
  starting transfers between devices  49 us (11%)
  blocking collectives  30.5 us (7%)
  local copies, waits for them, and re-layouts  27.4 us (6%)
  between operations  14 us (3%)
  other arithmetic  5.04 us (1%)
    ppermute x15, waiting for transfers between devices, shifted(): return lax.ppermute(block, axis, route)  89 us
    reduce_scatter x1, waiting for transfers between devices, local(): lax.psum_scatter((term + lax.dot_general(grad_up_pre, up_w, (((1,), (1,))...  53.8 us
    reduce_scatter x1, waiting for transfers between devices, local(): lax.psum_scatter(jnp.dot(hidden, down_w, preferred_element_type=jnp.float...  50.8 us
    all_gather x1, waiting for transfers between devices, local(): lax.all_gather(grad_arrived, 'ctx', axis=0, tiled=True)  30.2 us
    ppermute x15, starting transfers between devices, shifted(): return lax.ppermute(block, axis, route)  28.8 us
    all_to_all x1, blocking collectives, local(): lax.all_to_all(grad_slots.reshape(n_exp, capacity, width), 'exp', split_a...  16.9 us
    all_to_all x1, blocking collectives, local(): lax.all_to_all(send.reshape(n_exp, capacity, width), 'exp', split_axis=0,...  13.6 us
    all_gather x1, waiting for transfers between devices, local(): expert_in = lax.all_gather(arrived, 'ctx', axis=0, tiled=True)  12 us
  transfers between devices with their start and end apart: 22, of which 20 were waited for; matrix products, arithmetic and copies ran while one was open for 12% of the time, Pallas kernels for 0%

commit v1 on v0

--- a/solution.py
+++ b/solution.py
@@ -7,40 +7,12 @@
 masked_value = -1e30
 
 
-def shifted(block, axis, distance):
-    devices = range(lax.axis_size(axis))
-    route = [(i - distance, i) for i in devices if i - distance in devices]
-    return lax.ppermute(block, axis, route)
-
-
 def heads_first(query_local, group, head):
     count = query_local.shape[0]
     return query_local.reshape(count, group, head).transpose(1, 0, 2).reshape(group * count, head)
 
 
-def attend_piece(state, query_flat, query_pos, piece, start, head):
-    running_max, running_sum, accum = state
-    key_part = piece[:, :head]
-    value_part = piece[:, head:].astype(jnp.float32)
-    scores = lax.dot_general(
-        query_flat, key_part, (((1,), (1,)), ((), ())), preferred_element_type=jnp.float32
-    ) * head ** (-0.5)
-    key_pos = start + jnp.arange(piece.shape[0], dtype=jnp.int32)
-    allowed = key_pos[None, :] <= query_pos[:, None]
-    scores = jnp.where(allowed, scores, masked_value)
-    new_max = jnp.maximum(running_max, jnp.max(scores, axis=1))
-    weights = jnp.where(allowed, jnp.exp(scores - new_max[:, None]), 0.0)
-    factor = jnp.exp(running_max - new_max)
-    new_sum = running_sum * factor + jnp.sum(weights, axis=1)
-    product = jnp.dot(
-        weights, value_part, precision=lax.Precision.HIGHEST, preferred_element_type=jnp.float32
-    )
-    new_accum = accum * factor[:, None] + product
-    return (new_max, new_sum, new_accum)
-
-
 def local(queries, keys, values, norm_gain, routes, route_scores, cotangent, w_gate, w_up, w_down):
-    n_ctx = lax.axis_size("ctx")
     n_exp = lax.axis_size("exp")
     head = keys.shape[1]
     group = queries.shape[1] // head
@@ -48,25 +20,22 @@
     ctx_index = lax.axis_index("ctx")
     query_flat = heads_first(queries, group, head)
     query_pos = ctx_index * tok_ctx + jnp.tile(jnp.arange(tok_ctx, dtype=jnp.int32), group)
-    key_values = jnp.concatenate([keys, values], axis=1)
-    query_rows = query_flat.shape[0]
-    initial = (
-        jnp.full((query_rows,), masked_value, jnp.float32),
-        jnp.zeros((query_rows,), jnp.float32),
-        jnp.zeros((query_rows, head), jnp.float32),
+    key_values = lax.all_gather(
+        jnp.concatenate([keys, values], axis=1), "ctx", axis=0, tiled=True
     )
-    first = attend_piece(initial, query_flat, query_pos, key_values, ctx_index * tok_ctx, head)
-
-    def cycle_step(step, carry):
-        state, current = carry
-        current = shifted(current, "ctx", 1)
-        source = (ctx_index - step) % n_ctx
-        state = attend_piece(state, query_flat, query_pos, current, source * tok_ctx, head)
-        return (state, current)
-
-    state, _ = lax.fori_loop(1, n_ctx, cycle_step, (first, key_values))
-    running_max, running_sum, accum = state
-    attended = accum / running_sum[:, None]
+    scores = lax.dot_general(
+        query_flat, key_values[:, :head], (((1,), (1,)), ((), ())), preferred_element_type=jnp.float32
+    ) * head ** (-0.5)
+    allowed = jnp.arange(key_values.shape[0], dtype=jnp.int32)[None, :] <= query_pos[:, None]
+    scores = jnp.where(allowed, scores, masked_value)
+    weights = jnp.exp(scores - jnp.max(scores, axis=1, keepdims=True))
+    totals = jnp.sum(weights, axis=1, keepdims=True)
+    attended = (
+        jnp.dot(
+            weights.astype(jnp.bfloat16), key_values[:, head:], preferred_element_type=jnp.float32
+        )
+        / totals
+    )
     attended = (
         attended.reshape(group, tok_ctx, head)
         .transpose(1, 0, 2)
@@ -123,10 +92,8 @@
     grad_arrived = lax.all_to_all(
         grad_slots.reshape(n_exp, capacity, width), "exp", split_axis=0, concat_axis=0, tiled=True
     ).reshape(slots, width)
-    grad_out, rows_in = (
-        lax.all_gather(grad_arrived, "ctx", axis=0, tiled=True),
-        lax.all_gather(arrived, "ctx", axis=0, tiled=True),
-    )
+    grad_out = lax.all_gather(grad_arrived, "ctx", axis=0, tiled=True)
+    rows_in = expert_in
     grad_hidden = lax.dot_general(
         grad_out, down_w, (((1,), (1,)), ((), ())), preferred_element_type=jnp.float32
     )

time: 443 us -> 340 us (0.77)
  waiting for transfers between devices: 243 us -> 187 us
  starting transfers between devices: 49 us -> 19.2 us
  matrix products: 69.4 us -> 59.9 us
  local copies, waits for them, and re-layouts: 27.4 us -> 18.4 us
    ppermute x15 -> x0, waiting for transfers between devices: 89 us -> none  [shifted(): return lax.ppermute(block, axis, route)]
    all_gather x1 -> x2, waiting for transfers between devices: 30.2 us -> 61.1 us  [the longest x1 30.6 us: local(): lax.all_gather(jnp.concatenate([keys, values], axis=1), 'ctx', axis=0, ti...]
    ppermute x15 -> x0, starting transfers between devices: 28.8 us -> none  [shifted(): return lax.ppermute(block, axis, route)]
    while x30 -> x0, local copies, waits for them, and re-layouts: 9.51 us -> none
    dot_general x32 -> x2, matrix products: 11.9 us -> 2.42 us  [the longest x1 1.8 us: local(): lax.dot_general(query_flat, key_values[:, :head], (((1,), (1,)), ((), ())...]
  transfers between devices with their start and end apart: 22 -> 8, of which waited for: 20 -> 6; matrix products, arithmetic and copies ran while one was open for 12% -> 17% of each run, Pallas kernels for 0% -> 0%
where the time goes in v1:
time: 340 us; the launch traced here: 337 us
  waiting for transfers between devices  187 us (55%)
  matrix products  59.9 us (18%)
  blocking collectives  31.6 us (9%)
  starting transfers between devices  19.2 us (6%)
  local copies, waits for them, and re-layouts  18.4 us (5%)
  between operations  13.9 us (4%)
  other arithmetic  6.2 us (2%)
    reduce_scatter x1, waiting for transfers between devices, local(): lax.psum_scatter((term + lax.dot_general(grad_up_pre, up_w, (((1,), (1,))...  53.6 us
    reduce_scatter x1, waiting for transfers between devices, local(): lax.psum_scatter(jnp.dot(hidden, down_w, preferred_element_type=jnp.float...  50.8 us
    all_gather x1, waiting for transfers between devices, local(): lax.all_gather(jnp.concatenate([keys, values], axis=1), 'ctx', axis=0, ti...  30.6 us
    all_gather x1, waiting for transfers between devices, local(): grad_out = lax.all_gather(grad_arrived, 'ctx', axis=0, tiled=True)  30.5 us
    all_to_all x1, blocking collectives, local(): lax.all_to_all(grad_slots.reshape(n_exp, capacity, width), 'exp', split_a...  18.1 us
    all_gather x1, waiting for transfers between devices, local(): expert_in = lax.all_gather(arrived, 'ctx', axis=0, tiled=True)  14 us
    all_to_all x1, blocking collectives, local(): lax.all_to_all(send.reshape(n_exp, capacity, width), 'exp', split_axis=0,...  13.6 us
    all_to_all x1, waiting for transfers between devices, local(): lax.all_to_all(attended, 'exp', split_axis=0, concat_axis=1, tiled=True)  7.82 us
  transfers between devices with their start and end apart: 8, of which 6 were waited for; matrix products, arithmetic and copies ran while one was open for 17% of the time, Pallas kernels for 0%

profile of v1, /device:TPU:8, one launch (start us, length us, event | category | flops | bytes accessed | tf_op | source)
XLA Modules:
  0.0 336.8 jit_solution(3207125207926384056)
XLA Ops:
  7.2 0.0 all-gather.4.cloned.1.call-start
  7.2 1.6 pad_maximum_fusion
  8.8 0.0 all-gather.4.cloned.1.call-update
  8.8 0.8 copy.35
  9.6 0.1 eq.31
  9.7 0.1 fusion.30
  9.7 0.1 reduce_window_sum.11
  9.8 0.2 select_reduce_fusion.1
  10.0 0.1 reduce_sum.66
  10.1 0.1 copy.36
  10.2 1.0 copy.37
  11.2 0.1 copy.38
  11.3 0.7 reduce_max.18
  12.0 0.7 fusion.33
  12.7 0.7 fusion.32
  13.4 0.7 multiply_add_fusion
  14.1 30.6 %all-gather.4.cloned.1.call-done = bf16[2048,256]{1,0:T(8,128)(2,1)} async-done(((bf16[128,256]{1,0:T(8,128)(2,1)}), bf16[2048,256]{1,0:T(8,128)(2,1)}) %all-gather.4.cloned.1.call-update) | async-done | bytes 1048592 | tf_op jit(solution)/shard_map/all_gather | solution.py:23
  44.7 1.8 fusion.35
  46.5 0.5 fusion.13
  47.1 0.6 fusion.22
  47.7 0.1 copy.43
  47.8 0.7 convert_element_type.88
  48.5 6.0 %all-to-all-start = ((bf16[8,16,384]{2,1,0:T(8,128)(2,1)}), bf16[8,16,384]{2,1,0:T(8,128)(2,1)S(1)}, u32[]{:S(2)}, u32[]{:S(2)}) async-start(bf16[8,16,384]{2,1,0:T(8,128)(2,1)} %convert_element_type.88), calls=%async_computation | async-start | bytes 196608 | tf_op jit(solution)/shard_map/all_to_all | solution.py:45
  54.5 0.0 all-gather.6.cloned.1.call-start
  54.6 0.1 convert_reduce_fusion
  54.7 7.8 %all-to-all-done = bf16[8,16,384]{2,1,0:T(8,128)(2,1)S(1)} async-done(((bf16[8,16,384]{2,1,0:T(8,128)(2,1)}), bf16[8,16,384]{2,1,0:T(8,128)(2,1)S(1)}, u32[]{:S(2)}, u32[]{:S(2)}) %all-to-all-start) | async-done | bytes 98336 | tf_op jit(solution)/shard_map/all_to_all | solution.py:45
  62.5 0.1 fusion.27
  62.7 1.0 convolution_convert_fusion.5
  63.7 1.8 reshape.111
  65.5 13.6 %all_to_all.30 = bf16[8,6,3072]{2,1,0:T(8,128)(2,1)} all-to-all(bf16[8,6,3072]{2,1,0:T(8,128)(2,1)} %reshape.111), channel_id=1, replica_groups=mesh['ctx'=16,'exp'=8] {'exp'}, dimensions={0} | all-to-all | bytes 589824 | tf_op jit(solution)/shard_map/all_to_all | solution.py:64
  79.0 1.8 reshape.112
  80.9 0.0 all-gather.6.cloned.1.call-update
  80.9 0.0 all-gather.8.cloned.1.call-start
  80.9 1.2 convolution_convert_fusion.4
  82.1 1.8 reshape.115
  83.9 18.1 %all_to_all.31 = bf16[8,6,3072]{2,1,0:T(8,128)(2,1)} all-to-all(bf16[8,6,3072]{2,1,0:T(8,128)(2,1)} %reshape.115), channel_id=1, replica_groups=mesh['ctx'=16,'exp'=8] {'exp'}, dimensions={0} | all-to-all | bytes 589824 | tf_op jit(solution)/shard_map/all_to_all | solution.py:92
  102.0 1.8 reshape.116
  103.8 0.0 all-gather.8.cloned.1.call-update
  103.8 0.0 reduce-scatter.3.cloned.1.call-start
  103.8 14.0 %all-gather.6.cloned.1.call-done = bf16[768,3072]{1,0:T(8,128)(2,1)} async-done(((bf16[48,3072]{1,0:T(8,128)(2,1)}), bf16[768,3072]{1,0:T(8,128)(2,1)}) %all-gather.6.cloned.1.call-update) | async-done | bytes 4718608 | tf_op jit(solution)/shard_map/all_gather | solution.py:67
  117.8 7.2 %fusion.7 = f32[768,512]{1,0:T(8,128)} fusion(bf16[768,3072]{1,0:T(8,128)(2,1)} %all-gather.6.cloned.1.call-done, bf16[1,3072,512]{2,1,0:T(8,128)(2,1)} %param.18), kind=kOutput, calls=%fused_computation.16 | convolution fusion | flops 2415919104 | bytes 9437184 | tf_op jit(solution)/shard_map/dot_general | solution.py:72
  125.0 3.7 %fusion.11 = f32[768,512]{1,0:T(8,128)} fusion(bf16[768,3072]{1,0:T(8,128)(2,1)S(1)} %copy-done.6, bf16[1,3072,512]{2,1,0:T(8,128)(2,1)S(1)} %copy-done.7), kind=kOutput, calls=%fused_computation.20 | convolution fusion | flops 2415919104 | bytes 9437184 | tf_op jit(solution)/shard_map/dot_general | solution.py:71
  128.8 30.5 %all-gather.8.cloned.1.call-done = bf16[768,3072]{1,0:T(8,128)(2,1)} async-done(((bf16[48,3072]{1,0:T(8,128)(2,1)}), bf16[768,3072]{1,0:T(8,128)(2,1)}) %all-gather.8.cloned.1.call-update) | async-done | bytes 4718608 | tf_op jit(solution)/shard_map/all_gather | solution.py:95
  159.3 7.0 %multiply_convert_fusion = (bf16[768,512]{1,0:T(8,128)(2,1)}, bf16[768,512]{1,0:T(8,128)(2,1)}, bf16[768,512]{1,0:T(8,128)(2,1)S(1)}) fusion(f32[768,512]{1,0:T(8,128)} %fusion.11, f32[768,512]{1,0:T(8,128)} %fusion.7, bf16[768,3072]{1,0:T(8,128)(2,1)} %all-gather.8.cloned.1.call-done, bf16[1,512,3072]{2,1,0:T(8,128)(2,1)S(1)} %copy-done), kind=kOutput, calls=%fused_computation.28 | convolution fusion | flops 2421817344 | bytes 13369344 | tf_op jit(solution)/shard_map/dot_general | solution.py:97
  166.3 0.9 copy-done.8
  167.2 4.2 %convolution_convert_fusion = bf16[768,3072]{1,0:T(8,128)(2,1)} fusion(bf16[768,512]{1,0:T(8,128)(2,1)S(1)} %get-tuple-element.9, bf16[1,512,3072]{2,1,0:T(8,128)(2,1)S(1)} %copy-done), kind=kOutput, calls=%fused_computation.1 | convolution fusion | flops 2418278400 | bytes 8650752 | tf_op jit(solution)/shard_map/dot_general | solution.py:75
  171.4 0.0 reduce-scatter.3.cloned.1.call-update
  171.4 0.2 reduce-scatter.5.cloned.1.call-start
  171.7 4.9 %fusion.9 = f32[768,3072]{1,0:T(8,128)S(1)} fusion(bf16[768,512]{1,0:T(8,128)(2,1)} %get-tuple-element.8, bf16[1,3072,512]{2,1,0:T(8,128)(2,1)} %param.17), kind=kOutput, calls=%fused_computation.18 | convolution fusion | flops 2415919104 | bytes 13369344 | tf_op jit(solution)/shard_map/dot_general | solution.py:114
  176.6 4.4 %add_convert_fusion = bf16[768,3072]{1,0:T(8,128)(2,1)} fusion(f32[768,3072]{1,0:T(8,128)S(1)} %fusion.9, bf16[768,512]{1,0:T(8,128)(2,1)S(1)} %copy-done.2, bf16[1,3072,512]{2,1,0:T(8,128)(2,1)S(1)} %copy-done.1), kind=kOutput, calls=%fused_computation | convolution fusion | flops 2420637696 | bytes 18087936 | tf_op jit(solution)/shard_map/dot_general | solution.py:120
  181.1 6.9 %fusion.2 = bf16[1,512,3072]{2,1,0:T(8,128)(2,1)} fusion(bf16[768,512]{1,0:T(8,128)(2,1)} %copy-done.8, bf16[768,3072]{1,0:T(8,128)(2,1)} %all-gather.8.cloned.1.call-done), kind=kOutput, calls=%fused_computation.7 | convolution fusion | flops 2417491968 | bytes 8650752 | tf_op jit(solution)/shard_map/dot_general | solution.py:100
  188.0 50.8 %reduce-scatter.3.cloned.1.call-done = bf16[48,3072]{1,0:T(8,128)(2,1)} async-done(((bf16[768,3072]{1,0:T(8,128)(2,1)}), bf16[48,3072]{1,0:T(8,128)(2,1)}) %reduce-scatter.3.cloned.1.call-update) | async-done | bytes 294928 | tf_op jit(solution)/shard_map/reduce_scatter | solution.py:74
  238.8 1.8 reshape.113
  240.6 6.4 %all-to-all-start.2 = ((bf16[8,6,3072]{2,1,0:T(8,128)(2,1)}), bf16[8,6,3072]{2,1,0:T(8,128)(2,1)}, u32[]{:S(2)}, u32[]{:S(2)}) async-start(bf16[8,6,3072]{2,1,0:T(8,128)(2,1)} %reshape.113), calls=%async_computation.3 | async-start | bytes 786432 | tf_op jit(solution)/shard_map/all_to_all | solution.py:80
  247.1 6.9 %fusion.1 = bf16[1,3072,512]{2,1,0:T(8,128)(2,1)} fusion(bf16[768,3072]{1,0:T(8,128)(2,1)} %all-gather.6.cloned.1.call-done, bf16[768,512]{1,0:T(8,128)(2,1)} %get-tuple-element.7), kind=kOutput, calls=%fused_computation.6 | convolution fusion | flops 2417491968 | bytes 8650752 | tf_op jit(solution)/shard_map/dot_general | solution.py:111
  254.0 53.6 %reduce-scatter.5.cloned.1.call-done = bf16[48,3072]{1,0:T(8,128)(2,1)} async-done(((bf16[768,3072]{1,0:T(8,128)(2,1)}), bf16[48,3072]{1,0:T(8,128)(2,1)}) %reduce-scatter.5.cloned.1.call-update) | async-done | bytes 294928 | tf_op jit(solution)/shard_map/reduce_scatter | solution.py:117
  307.6 1.8 reshape.117
  309.4 6.4 %all-to-all-start.4 = ((bf16[8,6,3072]{2,1,0:T(8,128)(2,1)}), bf16[8,6,3072]{2,1,0:T(8,128)(2,1)}, u32[]{:S(2)}, u32[]{:S(2)}) async-start(bf16[8,6,3072]{2,1,0:T(8,128)(2,1)} %reshape.117), calls=%async_computation.6 | async-start | bytes 786432 | tf_op jit(solution)/shard_map/all_to_all | solution.py:128
  315.8 6.9 %fusion = bf16[1,3072,512]{2,1,0:T(8,128)(2,1)} fusion(bf16[768,3072]{1,0:T(8,128)(2,1)} %all-gather.6.cloned.1.call-done, bf16[768,512]{1,0:T(8,128)(2,1)} %get-tuple-element.8), kind=kOutput, calls=%fused_computation.5 | convolution fusion | flops 2417491968 | bytes 8650752 | tf_op jit(solution)/shard_map/dot_general | solution.py:108
  322.7 1.8 reshape.114
  324.5 1.9 convolution_convert_fusion.6
  326.4 1.8 reshape.118
  328.2 1.3 multiply_reduce_fusion
  329.5 0.7 subtract_convert_fusion
  (25 shorter events, 0.1 us)
Async XLA Ops:
  7.2 152.1 %copy-start = (bf16[1,512,3072]{2,1,0:T(8,128)(2,1)S(1)}, bf16[1,512,3072]{2,1,0:T(8,128)(2,1)}, u32[]{:S(2)}) copy-start(bf16[1,512,3072]{2,1,0:T(8,128)(2,1)} %param.19) | copy-start | bytes 9437188
  7.2 37.5 %all-gather.4.cloned.1.call-start = ((), (), s32[]{:S(2)}) async-start(), calls=%async_computation.7 | async-start | bytes 1114112 | tf_op jit(solution)/shard_map/all_gather | solution.py:23
  44.7 2.3 copy-start.3
  47.1 15.6 %copy-start.5 = (f32[3072]{0:T(1024)S(1)}, f32[3072]{0:T(1024)}, u32[]{:S(2)}) copy-start(f32[3072]{0:T(1024)} %param.13) | copy-start | bytes 36868
  47.7 33.2 %copy-start.4 = (bf16[16,3072]{1,0:T(8,128)(2,1)S(1)}, bf16[16,3072]{1,0:T(8,128)(2,1)}, u32[]{:S(2)}) copy-start(bf16[16,3072]{1,0:T(8,128)(2,1)} %param.16) | copy-start | bytes 294916
  48.5 13.9 %all-to-all-start = ((bf16[8,16,384]{2,1,0:T(8,128)(2,1)}), bf16[8,16,384]{2,1,0:T(8,128)(2,1)S(1)}, u32[]{:S(2)}, u32[]{:S(2)}) async-start(bf16[8,16,384]{2,1,0:T(8,128)(2,1)} %convert_element_type.88), calls=%async_computation | async-start | bytes 196608 | tf_op jit(solution)/shard_map/all_to_all | solution.py:45
  54.5 63.3 %all-gather.6.cloned.1.call-start = ((), (), s32[]{:S(2)}) async-start(), calls=%async_computation.8 | async-start | bytes 5013504 | tf_op jit(solution)/shard_map/all_gather | solution.py:67
  80.9 78.4 %all-gather.8.cloned.1.call-start = ((), (), s32[]{:S(2)}) async-start(), calls=%async_computation.10 | async-start | bytes 5013504 | tf_op jit(solution)/shard_map/all_gather | solution.py:95
  103.8 135.0 %reduce-scatter.3.cloned.1.call-start = ((), (), s32[]{:S(2)}) async-start(), calls=%async_computation.9 | async-start | bytes 5013504 | tf_op jit(solution)/shard_map/reduce_scatter | solution.py:74
  117.8 7.2 %copy-start.6 = (bf16[768,3072]{1,0:T(8,128)(2,1)S(1)}, bf16[768,3072]{1,0:T(8,128)(2,1)}, u32[]{:S(2)}) copy-start(bf16[768,3072]{1,0:T(8,128)(2,1)} %all-gather.6.cloned.1.call-done) | copy-start | bytes 14155780
  117.8 7.2 %copy-start.7 = (bf16[1,3072,512]{2,1,0:T(8,128)(2,1)S(1)}, bf16[1,3072,512]{2,1,0:T(8,128)(2,1)}, u32[]{:S(2)}) copy-start(bf16[1,3072,512]{2,1,0:T(8,128)(2,1)} %param.17) | copy-start | bytes 9437188
  166.3 0.9 copy-start.8
  171.4 136.1 %reduce-scatter.5.cloned.1.call-start = ((), (), s32[]{:S(2)}) async-start(), calls=%async_computation.11 | async-start | bytes 5013504 | tf_op jit(solution)/shard_map/reduce_scatter | solution.py:117
  171.7 4.9 %copy-start.1 = (bf16[1,3072,512]{2,1,0:T(8,128)(2,1)S(1)}, bf16[1,3072,512]{2,1,0:T(8,128)(2,1)}, u32[]{:S(2)}) copy-start(bf16[1,3072,512]{2,1,0:T(8,128)(2,1)} %param.18) | copy-start | bytes 9437188
  171.7 4.9 %copy-start.2 = (bf16[768,512]{1,0:T(8,128)(2,1)S(1)}, bf16[768,512]{1,0:T(8,128)(2,1)}, u32[]{:S(2)}) copy-start(bf16[768,512]{1,0:T(8,128)(2,1)} %get-tuple-element.7) | copy-start | bytes 2359300
  240.6 68.8 %all-to-all-start.2 = ((bf16[8,6,3072]{2,1,0:T(8,128)(2,1)}), bf16[8,6,3072]{2,1,0:T(8,128)(2,1)}, u32[]{:S(2)}, u32[]{:S(2)}) async-start(bf16[8,6,3072]{2,1,0:T(8,128)(2,1)} %reshape.113), calls=%async_computation.3 | async-start | bytes 786432 | tf_op jit(solution)/shard_map/all_to_all | solution.py:80
  309.4 17.0 %all-to-all-start.4 = ((bf16[8,6,3072]{2,1,0:T(8,128)(2,1)}), bf16[8,6,3072]{2,1,0:T(8,128)(2,1)}, u32[]{:S(2)}, u32[]{:S(2)}) async-start(bf16[8,6,3072]{2,1,0:T(8,128)(2,1)} %reshape.117), calls=%async_computation.6 | async-start | bytes 786432 | tf_op jit(solution)/shard_map/all_to_all | solution.py:128
Sparse Core Ops, SparseCore 0:
  10.3 34.3 all-gather.3
  81.0 36.7 all-gather.5
  120.1 39.1 all-gather.7
  171.5 67.2 reduce-scatter.2
  241.1 66.4 reduce-scatter.4

commit v2 on v1

--- a/solution.py
+++ b/solution.py
@@ -1,10 +1,408 @@
+import functools
+
 import jax
 import jax.numpy as jnp
 from jax import lax
+from jax.experimental import pallas as pl
+from jax.experimental.pallas import tpu as pltpu
 from jax.sharding import PartitionSpec as P
 
 norm_eps = 1e-05
 masked_value = -1e30
+NX, NY, NC = 4, 2, 2
+f32, bf16 = jnp.float32, jnp.bfloat16
+
+
+class Place:
+    def __init__(self):
+        c = lax.axis_index("ctx")
+        self.k = lax.rem(c, NC)
+        self.x = lax.rem(lax.div(c, NC), NX)
+        self.y = lax.div(c, NC * NX)
+        self.ok = 1 - self.k
+        self.oy = 1 - self.y
+        self.xr = lax.rem(self.x + 1, NX)
+        self.xl = lax.rem(self.x + 3, NX)
+        self.xf = lax.rem(self.x + 2, NX)
+        self.partner = self.index(self.x, self.y, self.ok)
+        self.across = self.index(self.x, self.oy, self.k)
+        self.right = self.index(self.xr, self.y, self.k)
+        self.left = self.index(self.xl, self.y, self.k)
+
+    def index(self, x, y, k):
+        return (y * NX + x) * NC + k
+
+
+class Copies:
+    def __init__(self, send, recv, tensor):
+        self.send, self.recv, self.tensor = send, recv, tensor
+        self.started, self.count = [], 0
+
+    def start(self, src, dst, device, arrival):
+        copy = pltpu.make_async_remote_copy(
+            src_ref=src, dst_ref=dst,
+            send_sem=self.send.at[self.tensor, self.count],
+            recv_sem=self.recv.at[self.tensor, arrival],
+            device_id={"ctx": device}, device_id_type=pl.DeviceIdType.MESH,
+        )
+        copy.start()
+        self.started.append(copy)
+        self.count += 1
+
+    def arrived(self, ref, arrival, device):
+        pltpu.make_async_remote_copy(
+            src_ref=ref, dst_ref=ref,
+            send_sem=self.send.at[self.tensor, 0],
+            recv_sem=self.recv.at[self.tensor, arrival],
+            device_id={"ctx": device}, device_id_type=pl.DeviceIdType.MESH,
+        ).wait_recv()
+
+    def drain(self):
+        for copy in self.started:
+            copy.wait_send()
+
+
+class Gather:
+    def __init__(self, copies, buf, rows, width, place):
+        self.c, self.buf, self.rows, self.width, self.p = copies, buf, rows, width, place
+
+    def block(self, x, y, k, half=None):
+        start = pl.multiple_of(((x * NY + y) * NC + k) * self.rows, 16)
+        if half is None:
+            return self.buf.at[pl.ds(start, self.rows), :]
+        mid = self.width // 2
+        return self.buf.at[pl.ds(start, self.rows), pl.ds(half * mid, mid)]
+
+    def send(self, ref, device, arrival):
+        self.c.start(ref, ref, device, arrival)
+
+    def own(self):
+        p = self.p
+        mine = self.block(p.x, p.y, p.k)
+        self.send(mine, p.across, 0)
+        self.send(mine, p.right, 1)
+        self.send(mine, p.left, 2)
+        self.send(mine, p.partner, 9)
+
+    def across(self):
+        p = self.p
+        got = self.block(p.x, p.oy, p.k)
+        self.c.arrived(got, 0, p.across)
+        self.send(got, p.right, 3)
+        self.send(got, p.left, 4)
+        self.send(got, p.partner, 10)
+
+    def beside(self, stage):
+        p = self.p
+        y = p.oy if stage else p.y
+        got = self.block(p.xl, y, p.k)
+        self.c.arrived(got, 1 + 2 * stage, p.left)
+        self.send(self.block(p.xl, y, p.k, 0), p.right, 5 + 2 * stage)
+        self.send(got, p.partner, 11 + 2 * stage)
+        got = self.block(p.xr, y, p.k)
+        self.c.arrived(got, 2 + 2 * stage, p.right)
+        self.send(self.block(p.xr, y, p.k, 1), p.left, 6 + 2 * stage)
+        self.send(got, p.partner, 12 + 2 * stage)
+
+    def far(self, stage):
+        p = self.p
+        y = p.oy if stage else p.y
+        self.c.arrived(self.block(p.xf, y, p.k, 0), 5 + 2 * stage, p.left)
+        self.c.arrived(self.block(p.xf, y, p.k, 1), 6 + 2 * stage, p.right)
+        self.send(self.block(p.xf, y, p.k), p.partner, 15 + stage)
+
+    def other_core(self, which):
+        p = self.p
+        spots = {
+            "own": [(p.x, p.y, 9), (p.x, p.oy, 10)],
+            "left": [(p.xl, p.y, 11), (p.xl, p.oy, 13)],
+            "right": [(p.xr, p.y, 12), (p.xr, p.oy, 14)],
+            "far": [(p.xf, p.y, 15), (p.xf, p.oy, 16)],
+        }[which]
+        for x, y, arrival in spots:
+            self.c.arrived(self.block(x, y, p.ok), arrival, p.partner)
+
+
+def add_into(dst, rows, count, width, first, sources):
+    step = 768
+
+    @pl.loop(0, width // step)
+    def _(i):
+        at = pl.multiple_of(i * step, 128)
+        spot = pl.multiple_of(first + i * step, 128)
+        total = dst[pl.ds(rows, count), pl.ds(spot, step)].astype(f32)
+        for source in sources:
+            total = total + source[:, pl.ds(at, step)].astype(f32)
+        dst[pl.ds(rows, count), pl.ds(spot, step)] = total.astype(bf16)
+
+
+class Reduce:
+    def __init__(self, copies, buf, core_in, far_in, near_in, across_in, rows, width, place):
+        self.c, self.buf, self.p, self.rows, self.width = copies, buf, place, rows, width
+        self.core_in, self.far_in, self.near_in, self.across_in = core_in, far_in, near_in, across_in
+
+    def start_of(self, x, y, k):
+        return pl.multiple_of(((x * NY + y) * NC + k) * self.rows, 16)
+
+    def block(self, x, y, k):
+        return self.buf.at[pl.ds(self.start_of(x, y, k), self.rows), :]
+
+    def half(self, x, y, k, half):
+        mid = self.width // 2
+        return self.buf.at[pl.ds(self.start_of(x, y, k), self.rows), pl.ds(half * mid, mid)]
+
+    def columns(self):
+        p = self.p
+        return [p.x, p.xr, p.xl, p.xf]
+
+    def core_send(self, which):
+        p = self.p
+        x = self.columns()[which]
+        for j, y in enumerate((p.oy, p.y)):
+            self.c.start(
+                self.block(x, y, p.ok), self.core_in.at[which, j], p.partner, which * 2 + j
+            )
+
+    def core_add(self, which):
+        p = self.p
+        x = self.columns()[which]
+        for j, y in enumerate((p.oy, p.y)):
+            self.c.arrived(self.core_in.at[which, j], which * 2 + j, p.partner)
+            add_into(
+                self.buf, self.start_of(x, y, p.k), self.rows, self.width, 0,
+                [self.core_in.at[which, j]],
+            )
+
+    def far_send(self):
+        p = self.p
+        for j, y in enumerate((p.oy, p.y)):
+            self.c.start(self.half(p.xf, y, p.k, 0), self.far_in.at[0, j], p.right, 8 + j)
+            self.c.start(self.half(p.xf, y, p.k, 1), self.far_in.at[1, j], p.left, 10 + j)
+
+    def near_send(self):
+        p = self.p
+        mid = self.width // 2
+        for j, y in enumerate((p.oy, p.y)):
+            self.c.arrived(self.far_in.at[0, j], 8 + j, p.left)
+            add_into(
+                self.buf, self.start_of(p.xr, y, p.k), self.rows, mid, 0, [self.far_in.at[0, j]]
+            )
+            self.c.start(self.block(p.xr, y, p.k), self.near_in.at[0, j], p.right, 12 + j)
+            self.c.arrived(self.far_in.at[1, j], 10 + j, p.right)
+            add_into(
+                self.buf, self.start_of(p.xl, y, p.k), self.rows, mid, mid, [self.far_in.at[1, j]]
+            )
+            self.c.start(self.block(p.xl, y, p.k), self.near_in.at[1, j], p.left, 14 + j)
+
+    def near_add(self, j):
+        p = self.p
+        y = (p.oy, p.y)[j]
+        self.c.arrived(self.near_in.at[0, j], 12 + j, p.left)
+        self.c.arrived(self.near_in.at[1, j], 14 + j, p.right)
+        add_into(
+            self.buf, self.start_of(p.x, y, p.k), self.rows, self.width, 0,
+            [self.near_in.at[0, j], self.near_in.at[1, j]],
+        )
+        if j == 0:
+            self.c.start(self.block(p.x, y, p.k), self.across_in, p.across, 16)
+
+    def finish(self):
+        p = self.p
+        self.c.arrived(self.across_in, 16, p.across)
+        add_into(
+            self.buf, self.start_of(p.x, p.y, p.k), self.rows, self.width, 0, [self.across_in]
+        )
+
+
+def dot(a, b, dims=((1,), (0,))):
+    return lax.dot_general(a, b, (dims, ((), ())), preferred_element_type=f32)
+
+
+def expert_kernel(
+    rows, width, hidden,
+    x_in, dy_in, wg_hbm, wu_hbm, wd_hbm,
+    y_out, dx_out, gg_out, gu_out, gd_out,
+    xbuf, dybuf, wg, wu, wd, hid, dgb, dub, py, px,
+    core_in, far_in, near_in, across_in, gg, gu, gd,
+    send, recv, local_sem,
+):
+    p = Place()
+    barrier = pltpu.get_barrier_semaphore()
+    for device in (p.partner, p.across, p.right, p.left):
+        pl.semaphore_signal(
+            barrier, inc=1, device_id={"ctx": device}, device_id_type=pl.DeviceIdType.MESH
+        )
+    loads = [
+        pltpu.make_async_copy(src, dst, local_sem.at[i])
+        for i, (src, dst) in enumerate(((wg_hbm, wg), (wu_hbm, wu), (wd_hbm, wd)))
+    ]
+    gx = Gather(Copies(send, recv, 0), xbuf, rows, width, p)
+    gy = Gather(Copies(send, recv, 1), dybuf, rows, width, p)
+    first = [
+        pltpu.make_async_copy(dy_in, gy.block(p.x, p.y, p.k), local_sem.at[3]),
+        pltpu.make_async_copy(x_in, gx.block(p.x, p.y, p.k), local_sem.at[4]),
+    ]
+    for copy in first + loads:
+        copy.start()
+    pl.semaphore_wait(barrier, 4)
+    first[0].wait()
+    gy.own()
+    first[1].wait()
+    gx.own()
+    gy.across()
+    gx.across()
+    for copy in loads:
+        copy.wait()
+    col = NY * NC * rows
+    tile = 256
+    wtile = 512
+
+    def first_half(x):
+        at = pl.multiple_of(x * col, 16)
+
+        @pl.loop(0, hidden // tile)
+        def _(n):
+            cols = pl.ds(pl.multiple_of(n * tile, 128), tile)
+            xs = xbuf[pl.ds(at, col), :]
+            g = dot(xs, wg[:, cols])
+            u = dot(xs, wu[:, cols])
+            dh = dot(dybuf[pl.ds(at, col), :], wd[pl.ds(pl.multiple_of(n * tile, 128), tile), :], ((1,), (1,)))
+            sig = 1.0 / (1.0 + jnp.exp(-g))
+            silu = g * sig
+            hid[pl.ds(at, col), cols] = (silu * u).astype(bf16)
+            dub[pl.ds(at, col), cols] = (dh * silu).astype(bf16)
+            dgb[pl.ds(at, col), cols] = (dh * u * sig * (1.0 + g * (1.0 - sig))).astype(bf16)
+
+    def second_half(x):
+        at = pl.multiple_of(x * col, 16)
+
+        @pl.loop(0, width // wtile)
+        def _(n):
+            spot = pl.ds(pl.multiple_of(n * wtile, 128), wtile)
+            py[pl.ds(at, col), spot] = dot(hid[pl.ds(at, col), :], wd[:, spot]).astype(bf16)
+            px[pl.ds(at, col), spot] = (
+                dot(dgb[pl.ds(at, col), :], wg[spot, :], ((1,), (1,)))
+                + dot(dub[pl.ds(at, col), :], wu[spot, :], ((1,), (1,)))
+            ).astype(bf16)
+
+    def weight_grads(begin, end):
+        @pl.loop(begin, end)
+        def _(n):
+            spot = pl.ds(pl.multiple_of(n * wtile, 128), wtile)
+            gd[:, spot] = dot(hid[...], dybuf[:, spot], ((0,), (0,))).astype(bf16)
+            xt = xbuf[:, spot]
+            gg[spot, :] = dot(xt, dgb[...], ((0,), (0,))).astype(bf16)
+            gu[spot, :] = dot(xt, dub[...], ((0,), (0,))).astype(bf16)
+            pltpu.make_async_copy(gd.at[:, spot], gd_out.at[:, spot], local_sem.at[5]).start()
+            pltpu.make_async_copy(gg.at[spot, :], gg_out.at[spot, :], local_sem.at[6]).start()
+            pltpu.make_async_copy(gu.at[spot, :], gu_out.at[spot, :], local_sem.at[7]).start()
+
+    ry = Reduce(Copies(send, recv, 2), py, core_in.at[0], far_in.at[0], near_in.at[0],
+                across_in.at[0], rows, width, p)
+    rx = Reduce(Copies(send, recv, 3), px, core_in.at[1], far_in.at[1], near_in.at[1],
+                across_in.at[1], rows, width, p)
+
+    def column(which, x):
+        first_half(x)
+        second_half(x)
+        ry.core_send(which)
+        rx.core_send(which)
+
+    gy.other_core("own")
+    gx.other_core("own")
+    gy.beside(0)
+    gx.beside(0)
+    column(0, p.x)
+    gy.beside(1)
+    gx.beside(1)
+    gy.far(0)
+    gx.far(0)
+    for side, which, x in (("right", 1, p.xr), ("left", 2, p.xl)):
+        gy.other_core(side)
+        gx.other_core(side)
+        column(which, x)
+    gy.far(1)
+    gx.far(1)
+    gy.other_core("far")
+    gx.other_core("far")
+    column(3, p.xf)
+    ry.core_add(3)
+    ry.far_send()
+    rx.core_add(3)
+    rx.far_send()
+    for which in (1, 2, 0):
+        ry.core_add(which)
+        rx.core_add(which)
+    weight_grads(0, 1)
+    ry.near_send()
+    weight_grads(1, 3)
+    rx.near_send()
+    weight_grads(3, width // wtile)
+    ry.near_add(0)
+    ry.near_add(1)
+    ry.finish()
+    rx.near_add(0)
+    rx.near_add(1)
+    rx.finish()
+    outs = [
+        pltpu.make_async_copy(ry.block(p.x, p.y, p.k), y_out, local_sem.at[3]),
+        pltpu.make_async_copy(rx.block(p.x, p.y, p.k), dx_out, local_sem.at[4]),
+    ]
+    for copy in outs:
+        copy.start()
+    for copy in outs:
+        copy.wait()
+    pltpu.make_async_copy(gd, gd_out, local_sem.at[5]).wait()
+    pltpu.make_async_copy(gg, gg_out, local_sem.at[6]).wait()
+    pltpu.make_async_copy(gu, gu_out, local_sem.at[7]).wait()
+    for work in (gx, gy, ry, rx):
+        work.c.drain()
+
+
+def experts(x_rows, dy_rows, gate_w, up_w, down_w):
+    rows, width = x_rows.shape
+    hidden = gate_w.shape[1]
+    total = rows * NX * NY * NC
+
+    hbm = pl.BlockSpec(memory_space=pl.ANY)
+    return pl.pallas_call(
+        functools.partial(expert_kernel, rows, width, hidden),
+        out_shape=(
+            jax.ShapeDtypeStruct((rows, width), bf16),
+            jax.ShapeDtypeStruct((rows, width), bf16),
+            jax.ShapeDtypeStruct(gate_w.shape, bf16),
+            jax.ShapeDtypeStruct(up_w.shape, bf16),
+            jax.ShapeDtypeStruct(down_w.shape, bf16),
+        ),
+        in_specs=[hbm] * 5,
+        out_specs=[hbm] * 5,
+        scratch_shapes=[
+            pltpu.VMEM((total, width), bf16),
+            pltpu.VMEM((total, width), bf16),
+            pltpu.VMEM(gate_w.shape, bf16),
+            pltpu.VMEM(up_w.shape, bf16),
+            pltpu.VMEM(down_w.shape, bf16),
+            pltpu.VMEM((total, hidden), bf16),
+            pltpu.VMEM((total, hidden), bf16),
+            pltpu.VMEM((total, hidden), bf16),
+            pltpu.VMEM((total, width), bf16),
+            pltpu.VMEM((total, width), bf16),
+            pltpu.VMEM((2, 4, 2, rows, width), bf16),
+            pltpu.VMEM((2, 2, 2, rows, width // 2), bf16),
+            pltpu.VMEM((2, 2, 2, rows, width), bf16),
+            pltpu.VMEM((2, rows, width), bf16),
+            pltpu.VMEM(gate_w.shape, bf16),
+            pltpu.VMEM(up_w.shape, bf16),
+            pltpu.VMEM(down_w.shape, bf16),
+            pltpu.SemaphoreType.DMA((4, 17)),
+            pltpu.SemaphoreType.DMA((4, 17)),
+            pltpu.SemaphoreType.DMA((8,)),
+        ],
+        compiler_params=pltpu.CompilerParams(
+            collective_id=0, has_side_effects=True, vmem_limit_bytes=66000000
+        ),
+        name="experts",
+    )(x_rows, dy_rows, gate_w, up_w, down_w)
 
 
 def heads_first(query_local, group, head):
@@ -64,18 +462,14 @@
     arrived = lax.all_to_all(
         send.reshape(n_exp, capacity, width), "exp", split_axis=0, concat_axis=0, tiled=True
     ).reshape(slots, width)
-    expert_in = lax.all_gather(arrived, "ctx", axis=0, tiled=True)
-    gate_w = w_gate[0]
-    up_w = w_up[0]
-    down_w = w_down[0]
-    gate_pre = jnp.dot(expert_in, gate_w, preferred_element_type=jnp.float32)
-    up_pre = jnp.dot(expert_in, up_w, preferred_element_type=jnp.float32)
-    hidden = (jax.nn.silu(gate_pre) * up_pre).astype(jnp.bfloat16)
-    expert_out = lax.psum_scatter(
-        jnp.dot(hidden, down_w, preferred_element_type=jnp.float32).astype(jnp.bfloat16),
-        "ctx",
-        scatter_dimension=0,
-        tiled=True,
+    grad_slots = jnp.dot(
+        mixing, cotangent.astype(jnp.float32), precision=lax.Precision.HIGHEST
+    ).astype(jnp.bfloat16)
+    grad_arrived = lax.all_to_all(
+        grad_slots.reshape(n_exp, capacity, width), "exp", split_axis=0, concat_axis=0, tiled=True
+    ).reshape(slots, width)
+    expert_out, grad_summed, grad_gate, grad_upw, grad_down = experts(
+        arrived, grad_arrived, w_gate[0], w_up[0], w_down[0]
     )
     returned = lax.all_to_all(
         expert_out.reshape(n_exp, capacity, width), "exp", split_axis=0, concat_axis=0, tiled=True
@@ -86,45 +480,6 @@
         (((0,), (0,)), ((), ())),
         precision=lax.Precision.HIGHEST,
     ).astype(jnp.bfloat16)
-    grad_slots = jnp.dot(
-        mixing, cotangent.astype(jnp.float32), precision=lax.Precision.HIGHEST
-    ).astype(jnp.bfloat16)
-    grad_arrived = lax.all_to_all(
-        grad_slots.reshape(n_exp, capacity, width), "exp", split_axis=0, concat_axis=0, tiled=True
-    ).reshape(slots, width)
-    grad_out = lax.all_gather(grad_arrived, "ctx", axis=0, tiled=True)
-    rows_in = expert_in
-    grad_hidden = lax.dot_general(
-        grad_out, down_w, (((1,), (1,)), ((), ())), preferred_element_type=jnp.float32
-    )
-    grad_down = lax.dot_general(
-        hidden, grad_out, (((0,), (0,)), ((), ())), preferred_element_type=jnp.float32
-    ).astype(jnp.bfloat16)
-    sig = jax.nn.sigmoid(gate_pre)
-    grad_up_pre = (grad_hidden * (gate_pre * sig)).astype(jnp.bfloat16)
-    grad_gate_pre = (grad_hidden * up_pre * sig * (1.0 + gate_pre * (1.0 - sig))).astype(
-        jnp.bfloat16
-    )
-    grad_gate = lax.dot_general(
-        rows_in, grad_gate_pre, (((0,), (0,)), ((), ())), preferred_element_type=jnp.float32
-    ).astype(jnp.bfloat16)
-    grad_upw = lax.dot_general(
-        rows_in, grad_up_pre, (((0,), (0,)), ((), ())), preferred_element_type=jnp.float32
-    ).astype(jnp.bfloat16)
-    term = lax.dot_general(
-        grad_gate_pre, gate_w, (((1,), (1,)), ((), ())), preferred_element_type=jnp.float32
-    )
-    grad_summed = lax.psum_scatter(
-        (
-            term
-            + lax.dot_general(
-                grad_up_pre, up_w, (((1,), (1,)), ((), ())), preferred_element_type=jnp.float32
-            )
-        ).astype(jnp.bfloat16),
-        "ctx",
-        scatter_dimension=0,
-        tiled=True,
-    )
     grad_back = lax.all_to_all(
         grad_summed.reshape(n_exp, capacity, width), "exp", split_axis=0, concat_axis=0, tiled=True
     ).reshape(slots, width)

time: 340 us -> 241 us (0.71)
  waiting for transfers between devices: 187 us -> 66.5 us
  Pallas kernels: 0 us -> 104 us
  matrix products: 59.9 us -> 6.3 us
  blocking collectives: 31.6 us -> 0 us
    reduce_scatter x2 -> x0, waiting for transfers between devices: 104 us -> none  [the longest x1 53.6 us: local(): lax.psum_scatter((term + lax.dot_general(grad_up_pre, up_w, (((1,), (1,))...]
    pallas_call x0 -> x1, Pallas kernels: none -> 104 us  [experts(): pl.pallas_call(functools.partial(expert_kernel, rows, width, hidden), out...]
    dot_general x9 -> x0, matrix products: 52.2 us -> none  [the longest x1 7.19 us: local(): up_pre = jnp.dot(expert_in, up_w, preferred_element_type=jnp.float32)]
    all_gather x2 -> x0, waiting for transfers between devices: 44.5 us -> none  [the longest x1 30.5 us: local(): grad_out = lax.all_gather(grad_arrived, 'ctx', axis=0, tiled=True)]
    all_to_all x2 -> x0, blocking collectives: 31.6 us -> none  [the longest x1 18.1 us: local(): lax.all_to_all(grad_slots.reshape(n_exp, capacity, width), 'exp', split_a...]
    all_to_all x0 -> x2, waiting for transfers between devices: none -> 16 us  [the longest x1 8.19 us: local(): lax.all_to_all(send.reshape(n_exp, capacity, width), 'exp', split_axis=0,...]
    all_to_all x1, waiting for transfers between devices: 0.01 us -> 7.46 us  [local(): lax.all_to_all(expert_out.reshape(n_exp, capacity, width), 'exp', split_a...]
    all_to_all x0 -> x2, starting transfers between devices: none -> 7.09 us  [the longest x1 3.63 us: local(): lax.all_to_all(send.reshape(n_exp, capacity, width), 'exp', split_axis=0,...]
  transfers between devices with their start and end apart: 8 -> 6, of which waited for: 6 -> 6; matrix products, arithmetic and copies ran while one was open for 17% -> 6% of each run, Pallas kernels for 0% -> 0%
where the time goes in v2:
time: 241 us; the launch traced here: 240 us
  Pallas kernels  104 us (43%)
  waiting for transfers between devices  66.5 us (28%)
  local copies, waits for them, and re-layouts  21.4 us (9%)
  starting transfers between devices  21.3 us (9%)
  between operations  14.2 us (6%)
  matrix products  6.3 us (3%)
  other arithmetic  6.04 us (3%)
    pallas_call x1, Pallas kernels, experts(): pl.pallas_call(functools.partial(expert_kernel, rows, width, hidden), out...  104 us
    all_gather x1, waiting for transfers between devices, local(): lax.all_gather(jnp.concatenate([keys, values], axis=1), 'ctx', axis=0, ti...  30.7 us
    unnamed x17, local copies, waits for them, and re-layouts  9.52 us
    all_to_all x1, waiting for transfers between devices, local(): lax.all_to_all(send.reshape(n_exp, capacity, width), 'exp', split_axis=0,...  8.19 us
    all_to_all x1, waiting for transfers between devices, local(): lax.all_to_all(grad_slots.reshape(n_exp, capacity, width), 'exp', split_a...  7.85 us
    all_to_all x1, waiting for transfers between devices, local(): lax.all_to_all(expert_out.reshape(n_exp, capacity, width), 'exp', split_a...  7.46 us
    all_to_all x1, waiting for transfers between devices, local(): lax.all_to_all(attended, 'exp', split_axis=0, concat_axis=1, tiled=True)  6.65 us
    all_to_all x1, starting transfers between devices, local(): lax.all_to_all(attended, 'exp', split_axis=0, concat_axis=1, tiled=True)  6 us
  transfers between devices with their start and end apart: 6, of which 6 were waited for; matrix products, arithmetic and copies ran while one was open for 6% of the time, Pallas kernels for 0%

profile of v2, /device:TPU:8, one launch (start us, length us, event | category | flops | bytes accessed | tf_op | source)
XLA Modules:
  0.0 239.6 jit_solution(15851232572092715928)
XLA Ops:
  7.2 0.0 copy-start
  7.2 0.0 all-gather.2.cloned.1.call-start
  7.2 1.4 pad_maximum_fusion
  8.6 0.0 all-gather.2.cloned.1.call-update
  8.7 0.8 copy.35
  9.4 0.1 eq.31
  9.5 0.1 fusion.16
  9.6 0.1 reduce_window_sum.11
  9.6 0.2 select_reduce_fusion.1
  9.8 0.1 reduce_sum.66
  9.9 0.1 copy.36
  10.0 1.0 copy.37
  11.0 0.1 copy.38
  11.2 0.7 reduce_max.18
  11.9 0.7 fusion.19
  12.6 0.7 fusion.18
  13.3 0.7 multiply_add_fusion
  13.9 0.1 convert_reduce_fusion
  14.0 30.7 %all-gather.2.cloned.1.call-done = bf16[2048,256]{1,0:T(8,128)(2,1)} async-done(((bf16[128,256]{1,0:T(8,128)(2,1)}), bf16[2048,256]{1,0:T(8,128)(2,1)}) %all-gather.2.cloned.1.call-update) | async-done | bytes 1048592 | tf_op jit(solution)/shard_map/all_gather | solution.py:421
  44.7 0.0 copy-start.4
  44.7 1.8 fusion.21
  46.5 0.5 fusion
  47.1 0.0 copy-done.4
  47.1 0.0 copy-start.5
  47.1 0.6 fusion.8
  47.7 0.1 copy.43
  47.8 0.7 convert_element_type.64
  48.5 6.0 %all-to-all-start = ((bf16[8,16,384]{2,1,0:T(8,128)(2,1)}), bf16[8,16,384]{2,1,0:T(8,128)(2,1)S(1)}, u32[]{:S(2)}, u32[]{:S(2)}) async-start(bf16[8,16,384]{2,1,0:T(8,128)(2,1)} %convert_element_type.64), calls=%async_computation | async-start | bytes 196608 | tf_op jit(solution)/shard_map/all_to_all | solution.py:443
  54.5 0.0 copy-done
  54.5 0.4 convolution_convert_fusion
  55.0 0.8 reshape.113
  55.8 6.6 %all-to-all-done = bf16[8,16,384]{2,1,0:T(8,128)(2,1)S(1)} async-done(((bf16[8,16,384]{2,1,0:T(8,128)(2,1)}), bf16[8,16,384]{2,1,0:T(8,128)(2,1)S(1)}, u32[]{:S(2)}, u32[]{:S(2)}) %all-to-all-start) | async-done | bytes 98336 | tf_op jit(solution)/shard_map/all_to_all | solution.py:443
  62.5 3.5 %all-to-all-start.2 = ((bf16[8,6,3072]{2,1,0:T(8,128)(2,1)}), bf16[8,6,3072]{2,1,0:T(8,128)(2,1)S(1)}, u32[]{:S(2)}, u32[]{:S(2)}) async-start(bf16[8,6,3072]{2,1,0:T(8,128)(2,1)} %reshape.113), calls=%async_computation.2 | async-start | bytes 786432 | tf_op jit(solution)/shard_map/all_to_all | solution.py:468
  65.9 0.1 fusion.13
  66.1 0.0 copy-done.5
  66.1 0.3 convolution_convert_fusion.1
  66.4 0.8 reshape.111
  67.3 7.9 %all-to-all-done.2 = bf16[8,6,3072]{2,1,0:T(8,128)(2,1)S(1)} async-done(((bf16[8,6,3072]{2,1,0:T(8,128)(2,1)}), bf16[8,6,3072]{2,1,0:T(8,128)(2,1)S(1)}, u32[]{:S(2)}, u32[]{:S(2)}) %all-to-all-start.2) | async-done | bytes 294944 | tf_op jit(solution)/shard_map/all_to_all | solution.py:468
  75.1 3.6 %all-to-all-start.1 = ((bf16[8,6,3072]{2,1,0:T(8,128)(2,1)}), bf16[8,6,3072]{2,1,0:T(8,128)(2,1)S(1)}, u32[]{:S(2)}, u32[]{:S(2)}) async-start(bf16[8,6,3072]{2,1,0:T(8,128)(2,1)} %reshape.111), calls=%async_computation.1 | async-start | bytes 786432 | tf_op jit(solution)/shard_map/all_to_all | solution.py:462
  78.8 0.8 reshape.114.dy_in
  79.6 8.2 %all-to-all-done.1 = bf16[8,6,3072]{2,1,0:T(8,128)(2,1)S(1)} async-done(((bf16[8,6,3072]{2,1,0:T(8,128)(2,1)}), bf16[8,6,3072]{2,1,0:T(8,128)(2,1)S(1)}, u32[]{:S(2)}, u32[]{:S(2)}) %all-to-all-start.1) | async-done | bytes 294944 | tf_op jit(solution)/shard_map/all_to_all | solution.py:462
  87.8 0.8 reshape.112.x_in
  88.6 103.9 %experts.1 = (bf16[48,3072]{1,0:T(8,128)(2,1)}, bf16[48,3072]{1,0:T(8,128)(2,1)}, bf16[3072,512]{1,0:T(8,128)(2,1)}, bf16[3072,512]{1,0:T(8,128)(2,1)}, bf16[512,3072]{1,0:T(8,128)(2,1)}) custom-call(bf16[48,3072]{1,0:T(8,128)(2,1)} %reshape.112.x_in, bf16[48,3072]{1,0:T(8,128)(2,1)} %reshape.114.dy_in, bf16[3072,512]{1,0:T(8,128)(2,1)} %bitcast.29, ...), custom_call_target="tpu_custom_call" | custom-call | tf_op jit(solution)/shard_map/experts/pallas_call | solution.py:368
  192.5 0.0 copy-start.3
  192.5 2.0 reshape.115
  194.4 4.1 %all-to-all-start.3 = ((bf16[8,6,3072]{2,1,0:T(8,128)(2,1)}), bf16[8,6,3072]{2,1,0:T(8,128)(2,1)}, u32[]{:S(2)}, u32[]{:S(2)}) async-start(bf16[8,6,3072]{2,1,0:T(8,128)(2,1)} %reshape.115), calls=%async_computation.3 | async-start | bytes 786432 | tf_op jit(solution)/shard_map/all_to_all | solution.py:474
  198.5 1.8 reshape.117
  200.4 7.5 %all-to-all-done.3 = bf16[8,6,3072]{2,1,0:T(8,128)(2,1)} async-done(((bf16[8,6,3072]{2,1,0:T(8,128)(2,1)}), bf16[8,6,3072]{2,1,0:T(8,128)(2,1)}, u32[]{:S(2)}, u32[]{:S(2)}) %all-to-all-start.3) | async-done | bytes 294944 | tf_op jit(solution)/shard_map/all_to_all | solution.py:474
  207.8 4.1 %all-to-all-start.4 = ((bf16[8,6,3072]{2,1,0:T(8,128)(2,1)}), bf16[8,6,3072]{2,1,0:T(8,128)(2,1)}, u32[]{:S(2)}, u32[]{:S(2)}) async-start(bf16[8,6,3072]{2,1,0:T(8,128)(2,1)} %reshape.117), calls=%async_computation.4 | async-start | bytes 786432 | tf_op jit(solution)/shard_map/all_to_all | solution.py:483
  211.9 1.8 reshape.116
  213.7 1.9 convolution_convert_fusion.2
  215.6 5.6 %all-to-all-done.4 = bf16[8,6,3072]{2,1,0:T(8,128)(2,1)} async-done(((bf16[8,6,3072]{2,1,0:T(8,128)(2,1)}), bf16[8,6,3072]{2,1,0:T(8,128)(2,1)}, u32[]{:S(2)}, u32[]{:S(2)}) %all-to-all-start.4) | async-done | bytes 294944 | tf_op jit(solution)/shard_map/all_to_all | solution.py:483
  221.2 1.8 reshape.118
  223.0 1.3 multiply_reduce_fusion
  224.3 0.7 subtract_convert_fusion
  225.1 0.0 copy-done.3
  225.1 0.0 copy-start.2
  225.1 1.7 copy.47
  226.7 1.4 copy-done.2
  228.1 0.0 copy-start.1
  228.1 1.7 copy.48
  229.8 1.4 copy-done.1
  231.1 1.7 copy.49
  (5 shorter events, 0.1 us)
Async XLA Ops:
  7.2 47.4 %copy-start = (bf16[16,3072]{1,0:T(8,128)(2,1)S(1)}, bf16[16,3072]{1,0:T(8,128)(2,1)}, u32[]{:S(2)}) copy-start(bf16[16,3072]{1,0:T(8,128)(2,1)} %param.16) | copy-start | bytes 294916
  7.2 37.5 %all-gather.2.cloned.1.call-start = ((), (), s32[]{:S(2)}) async-start(), calls=%async_computation.5 | async-start | bytes 1114112 | tf_op jit(solution)/shard_map/all_gather | solution.py:421
  44.7 2.3 copy-start.4
  47.1 19.1 %copy-start.5 = (f32[3072]{0:T(1024)S(1)}, f32[3072]{0:T(1024)}, u32[]{:S(2)}) copy-start(f32[3072]{0:T(1024)} %param.13) | copy-start | bytes 36868
  48.5 13.9 %all-to-all-start = ((bf16[8,16,384]{2,1,0:T(8,128)(2,1)}), bf16[8,16,384]{2,1,0:T(8,128)(2,1)S(1)}, u32[]{:S(2)}, u32[]{:S(2)}) async-start(bf16[8,16,384]{2,1,0:T(8,128)(2,1)} %convert_element_type.64), calls=%async_computation | async-start | bytes 196608 | tf_op jit(solution)/shard_map/all_to_all | solution.py:443
  62.5 12.6 %all-to-all-start.2 = ((bf16[8,6,3072]{2,1,0:T(8,128)(2,1)}), bf16[8,6,3072]{2,1,0:T(8,128)(2,1)S(1)}, u32[]{:S(2)}, u32[]{:S(2)}) async-start(bf16[8,6,3072]{2,1,0:T(8,128)(2,1)} %reshape.113), calls=%async_computation.2 | async-start | bytes 786432 | tf_op jit(solution)/shard_map/all_to_all | solution.py:468
  75.1 12.6 %all-to-all-start.1 = ((bf16[8,6,3072]{2,1,0:T(8,128)(2,1)}), bf16[8,6,3072]{2,1,0:T(8,128)(2,1)S(1)}, u32[]{:S(2)}, u32[]{:S(2)}) async-start(bf16[8,6,3072]{2,1,0:T(8,128)(2,1)} %reshape.111), calls=%async_computation.1 | async-start | bytes 786432 | tf_op jit(solution)/shard_map/all_to_all | solution.py:462
  192.5 32.6 %copy-start.3 = (bf16[3072,512]{1,0:T(8,128)(2,1)S(1)}, bf16[3072,512]{1,0:T(8,128)(2,1)}, u32[]{:S(2)}) copy-start(bf16[3072,512]{1,0:T(8,128)(2,1)} %get-tuple-element.12) | copy-start | bytes 9437188
  194.4 13.4 %all-to-all-start.3 = ((bf16[8,6,3072]{2,1,0:T(8,128)(2,1)}), bf16[8,6,3072]{2,1,0:T(8,128)(2,1)}, u32[]{:S(2)}, u32[]{:S(2)}) async-start(bf16[8,6,3072]{2,1,0:T(8,128)(2,1)} %reshape.115), calls=%async_computation.3 | async-start | bytes 786432 | tf_op jit(solution)/shard_map/all_to_all | solution.py:474
  207.8 13.4 %all-to-all-start.4 = ((bf16[8,6,3072]{2,1,0:T(8,128)(2,1)}), bf16[8,6,3072]{2,1,0:T(8,128)(2,1)}, u32[]{:S(2)}, u32[]{:S(2)}) async-start(bf16[8,6,3072]{2,1,0:T(8,128)(2,1)} %reshape.117), calls=%async_computation.4 | async-start | bytes 786432 | tf_op jit(solution)/shard_map/all_to_all | solution.py:483
  225.1 3.0 %copy-start.2 = (bf16[3072,512]{1,0:T(8,128)(2,1)S(1)}, bf16[3072,512]{1,0:T(8,128)(2,1)}, u32[]{:S(2)}) copy-start(bf16[3072,512]{1,0:T(8,128)(2,1)} %get-tuple-element.13) | copy-start | bytes 9437188
  228.1 3.0 %copy-start.1 = (bf16[512,3072]{1,0:T(8,128)(2,1)S(1)}, bf16[512,3072]{1,0:T(8,128)(2,1)}, u32[]{:S(2)}) copy-start(bf16[512,3072]{1,0:T(8,128)(2,1)} %get-tuple-element.14) | copy-start | bytes 9437188
Sparse Core Ops, SparseCore 0:
  10.3 34.3 all-gather.1

commit v3 on v2

--- a/solution.py
+++ b/solution.py
@@ -34,8 +34,8 @@
 
 
 class Copies:
-    def __init__(self, send, recv, tensor):
-        self.send, self.recv, self.tensor = send, recv, tensor
+    def __init__(self, send, recv, tensor, axis="ctx"):
+        self.send, self.recv, self.tensor, self.axis = send, recv, tensor, axis
         self.started, self.count = [], 0
 
     def start(self, src, dst, device, arrival):
@@ -43,7 +43,7 @@
             src_ref=src, dst_ref=dst,
             send_sem=self.send.at[self.tensor, self.count],
             recv_sem=self.recv.at[self.tensor, arrival],
-            device_id={"ctx": device}, device_id_type=pl.DeviceIdType.MESH,
+            device_id={self.axis: device}, device_id_type=pl.DeviceIdType.MESH,
         )
         copy.start()
         self.started.append(copy)
@@ -54,7 +54,7 @@
             src_ref=ref, dst_ref=ref,
             send_sem=self.send.at[self.tensor, 0],
             recv_sem=self.recv.at[self.tensor, arrival],
-            device_id={"ctx": device}, device_id_type=pl.DeviceIdType.MESH,
+            device_id={self.axis: device}, device_id_type=pl.DeviceIdType.MESH,
         ).wait_recv()
 
     def drain(self):
@@ -121,6 +121,15 @@
         }[which]
         for x, y, arrival in spots:
             self.c.arrived(self.block(x, y, p.ok), arrival, p.partner)
+
+    def all_but_own(self):
+        self.across()
+        for stage in range(2):
+            self.beside(stage)
+        for stage in range(2):
+            self.far(stage)
+        for which in ("own", "left", "right", "far"):
+            self.other_core(which)
 
 
 def add_into(dst, rows, count, width, first, sources):
@@ -218,44 +227,227 @@
     return lax.dot_general(a, b, (dims, ((), ())), preferred_element_type=f32)
 
 
-def expert_kernel(
-    rows, width, hidden,
-    x_in, dy_in, wg_hbm, wu_hbm, wd_hbm,
-    y_out, dx_out, gg_out, gu_out, gd_out,
-    xbuf, dybuf, wg, wu, wd, hid, dgb, dub, py, px,
+class HeadGather:
+    def __init__(self, copies, buf, head, group, e):
+        self.c, self.buf, self.head, self.group = copies, buf, head, group
+        hi, z = lax.div(e, 4), lax.rem(e, 4)
+        other = 1 - hi
+        along = [lax.rem(z + d, 4) for d in (1, 3, 2)]
+        self.e = e
+        self.mirror = other * 4 + z
+        self.peers = [hi * 4 + a for a in along]
+        self.mirrors = [other * 4 + a for a in along]
+
+    def block(self, e, h):
+        spot = pl.multiple_of((e * self.group + h) * self.head, 128)
+        return self.buf.at[:, pl.ds(spot, self.head)]
+
+    def own(self, h):
+        mine = self.block(self.e, h)
+        self.c.start(mine, mine, self.mirror, h * 7)
+        for i, peer in enumerate(self.peers):
+            self.c.start(mine, mine, peer, h * 7 + 1 + i)
+
+    def relay(self, h):
+        got = self.block(self.mirror, h)
+        self.c.arrived(got, h * 7, self.mirror)
+        for i, peer in enumerate(self.peers):
+            self.c.start(got, got, peer, h * 7 + 4 + i)
+
+    def rest(self, h):
+        for i, j in enumerate((1, 0, 2)):
+            self.c.arrived(self.block(self.peers[j], h), h * 7 + 1 + i, self.peers[j])
+            self.c.arrived(self.block(self.mirrors[j], h), h * 7 + 4 + i, self.peers[j])
+
+
+class Exchange:
+    def __init__(self, copies, out, into, sem, e, n):
+        self.c, self.out, self.into, self.e, self.n = copies, out, into, e, n
+        self.kept = pltpu.make_async_copy(out.at[e], into.at[e], sem)
+
+    def start(self):
+        for d in range(1, self.n):
+            peer = lax.rem(self.e + d, self.n)
+            self.c.start(self.out.at[peer], self.into.at[self.e], peer, d - 1)
+        self.kept.start()
+
+    def finish(self):
+        self.kept.wait()
+        for d in range(1, self.n):
+            peer = lax.rem(self.e + self.n - d, self.n)
+            self.c.arrived(self.into.at[peer], d - 1, peer)
+
+
+def dot(a, b, dims=((1,), (0,))):
+    return lax.dot_general(a, b, (dims, ((), ())), preferred_element_type=f32)
+
+
+def iota(shape, axis):
+    return lax.broadcasted_iota(jnp.int32, shape, axis)
+
+
+def kernel(
+    rows, width, hidden, head, group, n_exp,
+    q_hbm, k_hbm, v_hbm, gain, routes, scores, cot_hbm, wg_hbm, wu_hbm, wd_hbm,
+    mixed_out, gi_out, gg_out, gu_out, gd_out,
+    xbuf, dybuf, wg, wu, wd, hid, dgb, dub, dhb, py, px,
     core_in, far_in, near_in, across_in, gg, gu, gd,
+    q, kv, attn, cot, slabs_out, slabs_in, spots_out, spots_in, place, mix_hi, mix_lo,
     send, recv, local_sem,
 ):
     p = Place()
+    e = lax.axis_index("exp")
+    mesh_id = pl.DeviceIdType.MESH
+    tok = q.shape[0]
+    tok_dev = cot.shape[0]
+    slot = 8
+    slots = n_exp * slot
     barrier = pltpu.get_barrier_semaphore()
     for device in (p.partner, p.across, p.right, p.left):
+        pl.semaphore_signal(barrier, inc=1, device_id={"ctx": device}, device_id_type=mesh_id)
+    for d in range(1, n_exp):
         pl.semaphore_signal(
-            barrier, inc=1, device_id={"ctx": device}, device_id_type=pl.DeviceIdType.MESH
+            barrier, inc=1, device_id={"exp": lax.rem(e + d, n_exp)}, device_id_type=mesh_id
         )
+
+    def copies(tensor, axis="ctx"):
+        return Copies(send, recv, tensor, axis)
+
+    gx = Gather(copies(0), xbuf, rows, width, p)
+    gy = Gather(copies(1), dybuf, rows, width, p)
+    ry = Reduce(copies(2), py, core_in.at[0], far_in.at[0], near_in.at[0],
+                across_in.at[0], rows, width, p)
+    rx = Reduce(copies(3), px, core_in.at[1], far_in.at[1], near_in.at[1],
+                across_in.at[1], rows, width, p)
+    gk = Gather(copies(4), kv, tok, 2 * head, p)
+    ga = HeadGather(copies(5, "exp"), attn, head, group, e)
+    grads_there = Exchange(copies(6, "exp"), slabs_out.at[0], slabs_in.at[0], local_sem.at[8], e, n_exp)
+    spots_there = Exchange(copies(7, "exp"), spots_out, spots_in, local_sem.at[9], e, n_exp)
+    y_back = Exchange(copies(8, "exp"), slabs_out.at[1], slabs_in.at[1], local_sem.at[10], e, n_exp)
+    dx_back = Exchange(copies(9, "exp"), slabs_out.at[2], slabs_in.at[2], local_sem.at[11], e, n_exp)
+
+    own = pl.ds(pl.multiple_of(((p.x * NY + p.y) * NC + p.k) * tok, 16), tok)
+    first = [
+        pltpu.make_async_copy(k_hbm, kv.at[own, pl.ds(0, head)], local_sem.at[0]),
+        pltpu.make_async_copy(v_hbm, kv.at[own, pl.ds(head, head)], local_sem.at[1]),
+        pltpu.make_async_copy(cot_hbm, cot, local_sem.at[2]),
+        pltpu.make_async_copy(q_hbm, q, local_sem.at[3]),
+    ]
     loads = [
-        pltpu.make_async_copy(src, dst, local_sem.at[i])
-        for i, (src, dst) in enumerate(((wg_hbm, wg), (wu_hbm, wu), (wd_hbm, wd)))
-    ]
-    gx = Gather(Copies(send, recv, 0), xbuf, rows, width, p)
-    gy = Gather(Copies(send, recv, 1), dybuf, rows, width, p)
-    first = [
-        pltpu.make_async_copy(dy_in, gy.block(p.x, p.y, p.k), local_sem.at[3]),
-        pltpu.make_async_copy(x_in, gx.block(p.x, p.y, p.k), local_sem.at[4]),
+        pltpu.make_async_copy(src, dst, local_sem.at[4 + i])
+        for i, (src, dst) in enumerate(((wd_hbm, wd), (wg_hbm, wg), (wu_hbm, wu)))
     ]
     for copy in first + loads:
         copy.start()
-    pl.semaphore_wait(barrier, 4)
+
+    lane = iota((tok_dev, slots), 1)
+    expert, order = lane >> 3, lane & 7
+    in_a = routes[:, 0:1] == expert
+    in_b = routes[:, 1:2] == expert
+    named = jnp.where(in_a | in_b, 1.0, 0.0)
+    earlier = jnp.where(iota((tok_dev, tok_dev), 1) < iota((tok_dev, tok_dev), 0), 1.0, 0.0)
+    rank = dot(earlier.astype(bf16), named.astype(bf16))
+    here = (named > 0.5) & (rank.astype(jnp.int32) == order)
+    top = jnp.max(scores[...], axis=1, keepdims=True)
+    odds_a, odds_b = jnp.exp(scores[:, 0:1] - top), jnp.exp(scores[:, 1:2] - top)
+    whole = odds_a + odds_b
+    mix = jnp.where(here, jnp.where(in_a, odds_a / whole, odds_b / whole), 0.0)
+    placed = jnp.where(here, 1.0, 0.0).astype(bf16)
+    upper = mix.astype(bf16)
+    lower = (mix - upper.astype(f32)).astype(bf16)
+    place[...] = placed
+    mix_hi[...] = upper
+    mix_lo[...] = lower
+    shift = jnp.where(
+        iota((tok_dev, tok), 1) == iota((tok_dev, tok), 0) + e * tok_dev, 1.0, 0.0
+    ).astype(bf16)
+    spots_out[...] = dot(placed, shift, ((0,), (0,))).reshape(n_exp, slot, tok)
+
+    pl.semaphore_wait(barrier, 3 + n_exp)
     first[0].wait()
+    first[1].wait()
+    gk.own()
+    spots_there.start()
+    first[2].wait()
+    chunk = 512
+
+    @pl.loop(0, width // chunk)
+    def _(n):
+        spot = pl.ds(pl.multiple_of(n * chunk, 128), chunk)
+        part = dot(mix_hi[...], cot[:, spot], ((0,), (0,))) + dot(mix_lo[...], cot[:, spot], ((0,), (0,)))
+        slabs_out[0, :, :, spot] = part.reshape(n_exp, slot, chunk).astype(bf16)
+
+    grads_there.start()
+    row, from_row = iota((rows, slots), 0), iota((rows, slots), 1)
+    source = (row * 43) >> 8
+    squeeze = jnp.where(from_row == source * slot + (row - source * 6), 1.0, 0.0).astype(bf16)
+    gk.across()
+    gk.beside(0)
+    gk.beside(1)
+    gk.far(0)
+    gk.far(1)
+    spots_there.finish()
+    pick = dot(squeeze, spots_in[...].reshape(slots, tok).astype(bf16)).astype(bf16)
+    grads_there.finish()
+    own_rows = pl.ds(pl.multiple_of(((p.x * NY + p.y) * NC + p.k) * rows, 16), rows)
+
+    @pl.loop(0, width // chunk)
+    def _(n):
+        spot = pl.ds(pl.multiple_of(n * chunk, 128), chunk)
+        slabs = slabs_in[0, :, :, spot].astype(f32).reshape(slots, chunk).astype(bf16)
+        dybuf[own_rows, spot] = dot(squeeze, slabs).astype(bf16)
+
     gy.own()
-    first[1].wait()
+    first[3].wait()
+    for which in ("own", "left", "right", "far"):
+        gk.other_core(which)
+    total_keys = kv.shape[0]
+    at = iota((1, total_keys), 1)
+    block = at // tok
+    key_pos = (((block >> 1) & 1) * NX * NC + (block >> 2) * NC + (block & 1)) * tok + at % tok
+    query_pos = lax.axis_index("ctx") * tok + iota((tok, 1), 0)
+    for h in range(group):
+        s = dot(q[:, h * head : (h + 1) * head], kv[:, 0:head], ((1,), (1,))) * head ** (-0.5)
+        s = jnp.where(key_pos <= query_pos, s, masked_value)
+        weights = jnp.exp(s - jnp.max(s, axis=1, keepdims=True))
+        total = jnp.sum(weights, axis=1, keepdims=True)
+        out = dot(weights.astype(bf16), kv[:, head : 2 * head]) / total
+        spot = pl.multiple_of((e * group + h) * head, 128)
+        attn[:, pl.ds(spot, head)] = out.astype(bf16)
+        ga.own(h)
+    for h in range(group):
+        ga.relay(h)
+    gy.across()
+    for h in range(group):
+        ga.rest(h)
+
+    def squares(n, total):
+        part = attn[:, pl.ds(pl.multiple_of(n * chunk, 128), chunk)].astype(f32)
+        return total + jnp.sum(part * part, axis=1, keepdims=True)
+
+    total = lax.fori_loop(0, width // chunk, squares, jnp.zeros((tok, 1), f32))
+    inv = lax.rsqrt(total / width + norm_eps)
+
+    @pl.loop(0, width // chunk)
+    def _(n):
+        spot = pl.ds(pl.multiple_of(n * chunk, 128), chunk)
+        normed = (attn[:, spot].astype(f32) * inv * gain[:, spot]).astype(bf16)
+        xbuf[own_rows, spot] = dot(pick, normed).astype(bf16)
+
     gx.own()
-    gy.across()
-    gx.across()
     for copy in loads:
         copy.wait()
     col = NY * NC * rows
     tile = 256
     wtile = 512
+
+    def back_half(x):
+        at = pl.multiple_of(x * col, 16)
+
+        @pl.loop(0, hidden // tile)
+        def _(n):
+            spot = pl.ds(pl.multiple_of(n * tile, 128), tile)
+            dhb[pl.ds(at, col), spot] = dot(dybuf[pl.ds(at, col), :], wd[spot, :], ((1,), (1,)))
 
     def first_half(x):
         at = pl.multiple_of(x * col, 16)
@@ -266,7 +458,7 @@
             xs = xbuf[pl.ds(at, col), :]
             g = dot(xs, wg[:, cols])
             u = dot(xs, wu[:, cols])
-            dh = dot(dybuf[pl.ds(at, col), :], wd[pl.ds(pl.multiple_of(n * tile, 128), tile), :], ((1,), (1,)))
+            dh = dhb[pl.ds(at, col), cols]
             sig = 1.0 / (1.0 + jnp.exp(-g))
             silu = g * sig
             hid[pl.ds(at, col), cols] = (silu * u).astype(bf16)
@@ -297,42 +489,58 @@
             pltpu.make_async_copy(gg.at[spot, :], gg_out.at[spot, :], local_sem.at[6]).start()
             pltpu.make_async_copy(gu.at[spot, :], gu_out.at[spot, :], local_sem.at[7]).start()
 
-    ry = Reduce(Copies(send, recv, 2), py, core_in.at[0], far_in.at[0], near_in.at[0],
-                across_in.at[0], rows, width, p)
-    rx = Reduce(Copies(send, recv, 3), px, core_in.at[1], far_in.at[1], near_in.at[1],
-                across_in.at[1], rows, width, p)
-
     def column(which, x):
         first_half(x)
         second_half(x)
         ry.core_send(which)
         rx.core_send(which)
 
+    def to_slabs(buf, which):
+        row, to_row = iota((slots, rows), 1), iota((slots, rows), 0)
+        source = (row * 43) >> 8
+        spread = jnp.where(to_row == source * slot + (row - source * 6), 1.0, 0.0).astype(bf16)
+
+        @pl.loop(0, width // chunk)
+        def _(n):
+            spot = pl.ds(pl.multiple_of(n * chunk, 128), chunk)
+            part = dot(spread, buf[own_rows, spot])
+            slabs_out[which, :, :, spot] = part.reshape(n_exp, slot, chunk).astype(bf16)
+
+    def from_slabs(which, spot):
+        return slabs_in[which, :, :, spot].astype(f32).reshape(slots, chunk).astype(bf16)
+
+    gy.beside(0)
+    gy.beside(1)
     gy.other_core("own")
+    back_half(p.x)
+    gy.far(0)
+    gx.across()
+    gy.other_core("right")
+    gy.other_core("left")
+    back_half(p.xr)
+    back_half(p.xl)
+    gy.far(1)
+    gx.beside(0)
     gx.other_core("own")
-    gy.beside(0)
-    gx.beside(0)
     column(0, p.x)
-    gy.beside(1)
+    gy.other_core("far")
+    back_half(p.xf)
     gx.beside(1)
-    gy.far(0)
+    gx.other_core("right")
+    column(1, p.xr)
     gx.far(0)
-    for side, which, x in (("right", 1, p.xr), ("left", 2, p.xl)):
-        gy.other_core(side)
-        gx.other_core(side)
-        column(which, x)
-    gy.far(1)
+    gx.other_core("left")
+    column(2, p.xl)
     gx.far(1)
-    gy.other_core("far")
+    for which in (1, 2, 0):
+        ry.core_add(which)
+        rx.core_add(which)
     gx.other_core("far")
     column(3, p.xf)
     ry.core_add(3)
     ry.far_send()
     rx.core_add(3)
     rx.far_send()
-    for which in (1, 2, 0):
-        ry.core_add(which)
-        rx.core_add(which)
     weight_grads(0, 1)
     ry.near_send()
     weight_grads(1, 3)
@@ -341,41 +549,60 @@
     ry.near_add(0)
     ry.near_add(1)
     ry.finish()
+    to_slabs(py, 1)
+    y_back.start()
     rx.near_add(0)
+    y_back.finish()
+
+    @pl.loop(0, width // chunk)
+    def _(n):
+        spot = pl.ds(pl.multiple_of(n * chunk, 128), chunk)
+        slabs = from_slabs(1, spot)
+        mixed_out[:, spot] = (dot(mix_hi[...], slabs) + dot(mix_lo[...], slabs)).astype(bf16)
+
     rx.near_add(1)
     rx.finish()
-    outs = [
-        pltpu.make_async_copy(ry.block(p.x, p.y, p.k), y_out, local_sem.at[3]),
-        pltpu.make_async_copy(rx.block(p.x, p.y, p.k), dx_out, local_sem.at[4]),
-    ]
-    for copy in outs:
-        copy.start()
-    for copy in outs:
-        copy.wait()
+    to_slabs(px, 2)
+    dx_back.start()
+    dx_back.finish()
+    mine = pl.ds(pl.multiple_of(e * tok_dev, 16), tok_dev)
+    feats = attn[mine, :].astype(f32)
+    inv_own = lax.rsqrt(jnp.sum(feats * feats, axis=1, keepdims=True) / width + norm_eps)
+    back = slabs_in[2].astype(f32).reshape(slots, width).astype(bf16)
+    weighted = dot(place[...], back) * gain[...]
+    inner = jnp.sum(weighted * feats, axis=1, keepdims=True) / width
+    gi_out[...] = (inv_own * weighted - feats * (inv_own * inv_own * inv_own * inner)).astype(bf16)
     pltpu.make_async_copy(gd, gd_out, local_sem.at[5]).wait()
     pltpu.make_async_copy(gg, gg_out, local_sem.at[6]).wait()
     pltpu.make_async_copy(gu, gu_out, local_sem.at[7]).wait()
-    for work in (gx, gy, ry, rx):
+    for work in (gx, gy, ry, rx, gk, ga, grads_there, spots_there, y_back, dx_back):
         work.c.drain()
 
 
-def experts(x_rows, dy_rows, gate_w, up_w, down_w):
-    rows, width = x_rows.shape
+def local(queries, keys, values, norm_gain, routes, route_scores, cotangent, w_gate, w_up, w_down):
+    n_exp = lax.axis_size("exp")
+    head = keys.shape[1]
+    group = queries.shape[1] // head
+    tok = queries.shape[0]
+    tok_dev, width = cotangent.shape
+    rows = 3 * tok_dev
+    gate_w, up_w, down_w = w_gate[0], w_up[0], w_down[0]
     hidden = gate_w.shape[1]
     total = rows * NX * NY * NC
-
+    slots = 8 * n_exp
     hbm = pl.BlockSpec(memory_space=pl.ANY)
-    return pl.pallas_call(
-        functools.partial(expert_kernel, rows, width, hidden),
+    vmem = pl.BlockSpec(memory_space=pltpu.VMEM)
+    mixed, grad_input, grad_gate, grad_upw, grad_down = pl.pallas_call(
+        functools.partial(kernel, rows, width, hidden, head, group, n_exp),
         out_shape=(
-            jax.ShapeDtypeStruct((rows, width), bf16),
-            jax.ShapeDtypeStruct((rows, width), bf16),
+            jax.ShapeDtypeStruct((tok_dev, width), bf16),
+            jax.ShapeDtypeStruct((tok_dev, width), bf16),
             jax.ShapeDtypeStruct(gate_w.shape, bf16),
             jax.ShapeDtypeStruct(up_w.shape, bf16),
             jax.ShapeDtypeStruct(down_w.shape, bf16),
         ),
-        in_specs=[hbm] * 5,
-        out_specs=[hbm] * 5,
+        in_specs=[hbm, hbm, hbm, vmem, vmem, vmem, hbm, hbm, hbm, hbm],
+        out_specs=[vmem, vmem, hbm, hbm, hbm],
         scratch_shapes=[
             pltpu.VMEM((total, width), bf16),
             pltpu.VMEM((total, width), bf16),
@@ -385,6 +612,7 @@
             pltpu.VMEM((total, hidden), bf16),
             pltpu.VMEM((total, hidden), bf16),
             pltpu.VMEM((total, hidden), bf16),
+            pltpu.VMEM((total, hidden), f32),
             pltpu.VMEM((total, width), bf16),
             pltpu.VMEM((total, width), bf16),
             pltpu.VMEM((2, 4, 2, rows, width), bf16),
@@ -394,105 +622,28 @@
             pltpu.VMEM(gate_w.shape, bf16),
             pltpu.VMEM(up_w.shape, bf16),
             pltpu.VMEM(down_w.shape, bf16),
-            pltpu.SemaphoreType.DMA((4, 17)),
-            pltpu.SemaphoreType.DMA((4, 17)),
-            pltpu.SemaphoreType.DMA((8,)),
+            pltpu.VMEM(queries.shape, bf16),
+            pltpu.VMEM((tok * NX * NY * NC, 2 * head), bf16),
+            pltpu.VMEM((tok, width), bf16),
+            pltpu.VMEM((tok_dev, width), bf16),
+            pltpu.VMEM((3, n_exp, 8, width), bf16),
+            pltpu.VMEM((3, n_exp, 8, width), bf16),
+            pltpu.VMEM((n_exp, 8, tok), f32),
+            pltpu.VMEM((n_exp, 8, tok), f32),
+            pltpu.VMEM((tok_dev, slots), bf16),
+            pltpu.VMEM((tok_dev, slots), bf16),
+            pltpu.VMEM((tok_dev, slots), bf16),
+            pltpu.SemaphoreType.DMA((10, 21)),
+            pltpu.SemaphoreType.DMA((10, 21)),
+            pltpu.SemaphoreType.DMA((12,)),
         ],
         compiler_params=pltpu.CompilerParams(
-            collective_id=0, has_side_effects=True, vmem_limit_bytes=66000000
+            collective_id=0, has_side_effects=True, vmem_limit_bytes=67000000
         ),
-        name="experts",
-    )(x_rows, dy_rows, gate_w, up_w, down_w)
-
-
-def heads_first(query_local, group, head):
-    count = query_local.shape[0]
-    return query_local.reshape(count, group, head).transpose(1, 0, 2).reshape(group * count, head)
-
-
-def local(queries, keys, values, norm_gain, routes, route_scores, cotangent, w_gate, w_up, w_down):
-    n_exp = lax.axis_size("exp")
-    head = keys.shape[1]
-    group = queries.shape[1] // head
-    tok_ctx = queries.shape[0]
-    ctx_index = lax.axis_index("ctx")
-    query_flat = heads_first(queries, group, head)
-    query_pos = ctx_index * tok_ctx + jnp.tile(jnp.arange(tok_ctx, dtype=jnp.int32), group)
-    key_values = lax.all_gather(
-        jnp.concatenate([keys, values], axis=1), "ctx", axis=0, tiled=True
-    )
-    scores = lax.dot_general(
-        query_flat, key_values[:, :head], (((1,), (1,)), ((), ())), preferred_element_type=jnp.float32
-    ) * head ** (-0.5)
-    allowed = jnp.arange(key_values.shape[0], dtype=jnp.int32)[None, :] <= query_pos[:, None]
-    scores = jnp.where(allowed, scores, masked_value)
-    weights = jnp.exp(scores - jnp.max(scores, axis=1, keepdims=True))
-    totals = jnp.sum(weights, axis=1, keepdims=True)
-    attended = (
-        jnp.dot(
-            weights.astype(jnp.bfloat16), key_values[:, head:], preferred_element_type=jnp.float32
-        )
-        / totals
-    )
-    attended = (
-        attended.reshape(group, tok_ctx, head)
-        .transpose(1, 0, 2)
-        .reshape(tok_ctx, group * head)
-        .astype(jnp.bfloat16)
-    )
-    features = lax.all_to_all(attended, "exp", split_axis=0, concat_axis=1, tiled=True)
-    feats = features.astype(jnp.float32)
-    inv_rms = lax.rsqrt(jnp.mean(feats * feats, axis=1) + norm_eps)
-    normed = (feats * inv_rms[:, None] * norm_gain[None, :]).astype(jnp.bfloat16)
-    tok_dev = normed.shape[0]
-    width = normed.shape[1]
-    capacity = 3 * tok_dev // n_exp
-    slots = n_exp * capacity
-    flat_routes = routes.reshape(-1)
-    onehot = (flat_routes[:, None] == jnp.arange(n_exp, dtype=jnp.int32)[None, :]).astype(jnp.int32)
-    ranks = jnp.sum((jnp.cumsum(onehot, axis=0) - onehot) * onehot, axis=1)
-    target = flat_routes * capacity + ranks
-    placed = (jnp.arange(slots, dtype=jnp.int32)[:, None] == target[None, :]).astype(jnp.float32)
-    place_tokens = placed.reshape(slots, tok_dev, 2).sum(axis=2)
-    probs = jax.nn.softmax(route_scores, axis=1)
-    mixing = (placed * probs.reshape(-1)[None, :]).reshape(slots, tok_dev, 2).sum(axis=2)
-    send = jnp.dot(
-        place_tokens.astype(jnp.bfloat16), normed, preferred_element_type=jnp.float32
-    ).astype(jnp.bfloat16)
-    arrived = lax.all_to_all(
-        send.reshape(n_exp, capacity, width), "exp", split_axis=0, concat_axis=0, tiled=True
-    ).reshape(slots, width)
-    grad_slots = jnp.dot(
-        mixing, cotangent.astype(jnp.float32), precision=lax.Precision.HIGHEST
-    ).astype(jnp.bfloat16)
-    grad_arrived = lax.all_to_all(
-        grad_slots.reshape(n_exp, capacity, width), "exp", split_axis=0, concat_axis=0, tiled=True
-    ).reshape(slots, width)
-    expert_out, grad_summed, grad_gate, grad_upw, grad_down = experts(
-        arrived, grad_arrived, w_gate[0], w_up[0], w_down[0]
-    )
-    returned = lax.all_to_all(
-        expert_out.reshape(n_exp, capacity, width), "exp", split_axis=0, concat_axis=0, tiled=True
-    ).reshape(slots, width)
-    mixed = lax.dot_general(
-        mixing,
-        returned.astype(jnp.float32),
-        (((0,), (0,)), ((), ())),
-        precision=lax.Precision.HIGHEST,
-    ).astype(jnp.bfloat16)
-    grad_back = lax.all_to_all(
-        grad_summed.reshape(n_exp, capacity, width), "exp", split_axis=0, concat_axis=0, tiled=True
-    ).reshape(slots, width)
-    grad_normed = lax.dot_general(
-        place_tokens,
-        grad_back.astype(jnp.float32),
-        (((0,), (0,)), ((), ())),
-        precision=lax.Precision.HIGHEST,
-    )
-    weighted = grad_normed * norm_gain[None, :]
-    inner = jnp.mean(weighted * feats, axis=1)
-    grad_input = (inv_rms[:, None] * weighted - feats * (inv_rms**3 * inner)[:, None]).astype(
-        jnp.bfloat16
+        name="layer",
+    )(
+        queries, keys, values, norm_gain.reshape(1, width), routes, route_scores, cotangent,
+        gate_w, up_w, down_w,
     )
     return (mixed, grad_input, grad_gate[None], grad_upw[None], grad_down[None])
 

time: 241 us -> 151 us (0.63)
  waiting for transfers between devices: 66.5 us -> 0 us
  Pallas kernels: 104 us -> 133 us
  starting transfers between devices: 21.3 us -> 0 us
  between operations: 14.2 us -> 0.64 us
  local copies, waits for them, and re-layouts: 21.4 us -> 14.4 us
  matrix products: 6.3 us -> 0 us
  other arithmetic: 6.04 us -> 0 us
    all_to_all x5 -> x0, waiting for transfers between devices: 35.8 us -> none  [the longest x1 8.19 us: local(): lax.all_to_all(send.reshape(n_exp, capacity, width), 'exp', split_axis=0,...]
    all_gather x1 -> x0, waiting for transfers between devices: 30.7 us -> none  [local(): lax.all_gather(jnp.concatenate([keys, values], axis=1), 'ctx', axis=0, ti...]
    pallas_call x1, Pallas kernels: 104 us -> 133 us  [local(): pl.pallas_call(functools.partial(kernel, rows, width, hidden, head, group...]
    all_to_all x5 -> x0, starting transfers between devices: 21.3 us -> none  [the longest x1 6 us: local(): lax.all_to_all(attended, 'exp', split_axis=0, concat_axis=1, tiled=True)]
    reshape x8 -> x0, local copies, waits for them, and re-layouts: 10.7 us -> none  [the longest x1 1.96 us: local(): expert_out.reshape(n_exp, capacity, width)]
    dot_general x6 -> x0, matrix products: 6.3 us -> none  [the longest x1 1.85 us: local(): lax.dot_general(mixing, returned.astype(jnp.float32), (((0,), (0,)), ((),...]
    unnamed x17 -> x11, local copies, waits for them, and re-layouts: 9.52 us -> 14.4 us
  transfers between devices with their start and end apart: 6 -> 0, of which waited for: 6 -> 0; matrix products, arithmetic and copies ran while one was open for 6% -> 0% of each run, Pallas kernels for 0% -> 0%
where the time goes in v3:
time: 151 us; the launch traced here: 148 us
  Pallas kernels  133 us (88%)
  local copies, waits for them, and re-layouts  14.4 us (10%)
    pallas_call x1, Pallas kernels, local(): pl.pallas_call(functools.partial(kernel, rows, width, hidden, head, group...  133 us
    unnamed x11, local copies, waits for them, and re-layouts  14.4 us

profile of v3, /device:TPU:8, one launch (start us, length us, event | category | flops | bytes accessed | tf_op | source)
XLA Modules:
  0.0 147.7 jit_solution(9335642147113938842)
XLA Ops:
  0.6 1.4 copy.15.routes
  2.0 1.4 copy.16.scores
  3.3 132.6 %layer.1 = (bf16[16,3072]{1,0:T(8,128)(2,1)}, bf16[16,3072]{1,0:T(8,128)(2,1)}, bf16[3072,512]{1,0:T(8,128)(2,1)}, bf16[3072,512]{1,0:T(8,128)(2,1)}, bf16[512,3072]{1,0:T(8,128)(2,1)}) custom-call(bf16[128,384]{1,0:T(8,128)(2,1)} %q_hbm.1, bf16[128,128]{1,0:T(8,128)(2,1)} %k_hbm.1, bf16[128,128]{1,0:T(8,128)(2,1)} %v_hbm.1, f32[1,3072]{1,0:T(1,128)} %bitcast.13, ...), custom_call_target="tpu_custom_call" | custom-call | tf_op jit(solution)/shard_map/layer/pallas_call | solution.py:595
  136.0 1.5 %copy.22 = bf16[16,3072]{1,0:T(8,128)(2,1)} copy(bf16[16,3072]{1,0:T(8,128)(2,1)} %get-tuple-element.20) | data formatting | bytes 196608
  137.5 1.5 %copy.23 = bf16[16,3072]{1,0:T(8,128)(2,1)} copy(bf16[16,3072]{1,0:T(8,128)(2,1)} %get-tuple-element.21) | data formatting | bytes 196608
  139.1 0.0 copy-start.1
  139.1 3.9 %copy.24 = bf16[1,3072,512]{2,1,0:T(8,128)(2,1)} copy(bf16[1,3072,512]{2,1,0:T(8,128)(2,1)} %bitcast.12) | data formatting | bytes 6291456
  143.0 0.0 copy-done.1
  143.0 0.0 copy-start
  143.0 1.7 %copy.25 = bf16[1,3072,512]{2,1,0:T(8,128)(2,1)} copy(bf16[1,3072,512]{2,1,0:T(8,128)(2,1)S(1)} %bitcast.11) | data formatting | bytes 6291456
  144.6 1.4 copy-done
  146.0 1.7 %copy.26 = bf16[1,512,3072]{2,1,0:T(8,128)(2,1)} copy(bf16[1,512,3072]{2,1,0:T(8,128)(2,1)S(1)} %bitcast.10) | data formatting | bytes 6291456
Async XLA Ops:
  139.1 3.9 %copy-start.1 = (bf16[3072,512]{1,0:T(8,128)(2,1)S(1)}, bf16[3072,512]{1,0:T(8,128)(2,1)}, u32[]{:S(2)}) copy-start(bf16[3072,512]{1,0:T(8,128)(2,1)} %get-tuple-element.13) | copy-start | bytes 9437188
  143.0 3.0 %copy-start = (bf16[512,3072]{1,0:T(8,128)(2,1)S(1)}, bf16[512,3072]{1,0:T(8,128)(2,1)}, u32[]{:S(2)}) copy-start(bf16[512,3072]{1,0:T(8,128)(2,1)} %get-tuple-element.14) | copy-start | bytes 9437188

commit v4 on v3

--- a/solution.py
+++ b/solution.py
@@ -63,8 +63,9 @@
 
 
 class Gather:
-    def __init__(self, copies, buf, rows, width, place):
+    def __init__(self, copies, buf, rows, width, place, over_y=False):
         self.c, self.buf, self.rows, self.width, self.p = copies, buf, rows, width, place
+        self.over_y = over_y
 
     def block(self, x, y, k, half=None):
         start = pl.multiple_of(((x * NY + y) * NC + k) * self.rows, 16)
@@ -97,18 +98,25 @@
         y = p.oy if stage else p.y
         got = self.block(p.xl, y, p.k)
         self.c.arrived(got, 1 + 2 * stage, p.left)
-        self.send(self.block(p.xl, y, p.k, 0), p.right, 5 + 2 * stage)
+        if not (stage and self.over_y):
+            self.send(self.block(p.xl, y, p.k, 0), p.right, 5 + 2 * stage)
         self.send(got, p.partner, 11 + 2 * stage)
         got = self.block(p.xr, y, p.k)
         self.c.arrived(got, 2 + 2 * stage, p.right)
-        self.send(self.block(p.xr, y, p.k, 1), p.left, 6 + 2 * stage)
+        if not (stage and self.over_y):
+            self.send(self.block(p.xr, y, p.k, 1), p.left, 6 + 2 * stage)
         self.send(got, p.partner, 12 + 2 * stage)
 
     def far(self, stage):
         p = self.p
         y = p.oy if stage else p.y
-        self.c.arrived(self.block(p.xf, y, p.k, 0), 5 + 2 * stage, p.left)
-        self.c.arrived(self.block(p.xf, y, p.k, 1), 6 + 2 * stage, p.right)
+        if stage and self.over_y:
+            self.c.arrived(self.block(p.xf, y, p.k), 7, p.across)
+        else:
+            self.c.arrived(self.block(p.xf, y, p.k, 0), 5 + 2 * stage, p.left)
+            self.c.arrived(self.block(p.xf, y, p.k, 1), 6 + 2 * stage, p.right)
+        if self.over_y and not stage:
+            self.send(self.block(p.xf, y, p.k), p.across, 7)
         self.send(self.block(p.xf, y, p.k), p.partner, 15 + stage)
 
     def other_core(self, which):
@@ -146,9 +154,12 @@
 
 
 class Reduce:
-    def __init__(self, copies, buf, core_in, far_in, near_in, across_in, rows, width, place):
+    def __init__(
+        self, copies, buf, core_in, far_in, near_in, across_in, far_across_in, rows, width, place
+    ):
         self.c, self.buf, self.p, self.rows, self.width = copies, buf, place, rows, width
         self.core_in, self.far_in, self.near_in, self.across_in = core_in, far_in, near_in, across_in
+        self.far_across_in = far_across_in
 
     def start_of(self, x, y, k):
         return pl.multiple_of(((x * NY + y) * NC + k) * self.rows, 16)
@@ -182,26 +193,33 @@
                 [self.core_in.at[which, j]],
             )
 
+    def near_early(self, side):
+        p = self.p
+        x, device = ((p.xr, p.right), (p.xl, p.left))[side]
+        self.c.start(self.block(x, p.oy, p.k), self.near_in.at[side, 0], device, 12 + 2 * side)
+
+    def far_across(self):
+        p = self.p
+        self.c.start(self.block(p.xf, p.oy, p.k), self.far_across_in, p.across, 17)
+
     def far_send(self):
         p = self.p
-        for j, y in enumerate((p.oy, p.y)):
-            self.c.start(self.half(p.xf, y, p.k, 0), self.far_in.at[0, j], p.right, 8 + j)
-            self.c.start(self.half(p.xf, y, p.k, 1), self.far_in.at[1, j], p.left, 10 + j)
+        self.c.arrived(self.far_across_in, 17, p.across)
+        add_into(
+            self.buf, self.start_of(p.xf, p.y, p.k), self.rows, self.width, 0, [self.far_across_in]
+        )
+        self.c.start(self.half(p.xf, p.y, p.k, 0), self.far_in.at[0], p.right, 8)
+        self.c.start(self.half(p.xf, p.y, p.k, 1), self.far_in.at[1], p.left, 9)
 
     def near_send(self):
         p = self.p
         mid = self.width // 2
-        for j, y in enumerate((p.oy, p.y)):
-            self.c.arrived(self.far_in.at[0, j], 8 + j, p.left)
-            add_into(
-                self.buf, self.start_of(p.xr, y, p.k), self.rows, mid, 0, [self.far_in.at[0, j]]
-            )
-            self.c.start(self.block(p.xr, y, p.k), self.near_in.at[0, j], p.right, 12 + j)
-            self.c.arrived(self.far_in.at[1, j], 10 + j, p.right)
-            add_into(
-                self.buf, self.start_of(p.xl, y, p.k), self.rows, mid, mid, [self.far_in.at[1, j]]
-            )
-            self.c.start(self.block(p.xl, y, p.k), self.near_in.at[1, j], p.left, 14 + j)
+        self.c.arrived(self.far_in.at[0], 8, p.left)
+        add_into(self.buf, self.start_of(p.xr, p.y, p.k), self.rows, mid, 0, [self.far_in.at[0]])
+        self.c.start(self.block(p.xr, p.y, p.k), self.near_in.at[0, 1], p.right, 13)
+        self.c.arrived(self.far_in.at[1], 9, p.right)
+        add_into(self.buf, self.start_of(p.xl, p.y, p.k), self.rows, mid, mid, [self.far_in.at[1]])
+        self.c.start(self.block(p.xl, p.y, p.k), self.near_in.at[1, 1], p.left, 15)
 
     def near_add(self, j):
         p = self.p
@@ -231,33 +249,46 @@
     def __init__(self, copies, buf, head, group, e):
         self.c, self.buf, self.head, self.group = copies, buf, head, group
         hi, z = lax.div(e, 4), lax.rem(e, 4)
-        other = 1 - hi
-        along = [lax.rem(z + d, 4) for d in (1, 3, 2)]
+        up, down, far = [lax.rem(z + d, 4) for d in (1, 3, 2)]
         self.e = e
-        self.mirror = other * 4 + z
-        self.peers = [hi * 4 + a for a in along]
-        self.mirrors = [other * 4 + a for a in along]
-
-    def block(self, e, h):
+        self.mirror = (1 - hi) * 4 + z
+        self.up, self.down = hi * 4 + up, hi * 4 + down
+        self.ups = [self.up, (1 - hi) * 4 + up]
+        self.downs = [self.down, (1 - hi) * 4 + down]
+        self.fars = [hi * 4 + far, (1 - hi) * 4 + far]
+
+    def block(self, e, h, half=None):
         spot = pl.multiple_of((e * self.group + h) * self.head, 128)
-        return self.buf.at[:, pl.ds(spot, self.head)]
+        if half is None:
+            return self.buf.at[:, pl.ds(spot, self.head)]
+        count = self.buf.shape[0] // 2
+        return self.buf.at[pl.ds(half * count, count), pl.ds(spot, self.head)]
 
     def own(self, h):
         mine = self.block(self.e, h)
-        self.c.start(mine, mine, self.mirror, h * 7)
-        for i, peer in enumerate(self.peers):
-            self.c.start(mine, mine, peer, h * 7 + 1 + i)
+        self.c.start(mine, mine, self.mirror, h * 9)
+        self.c.start(mine, mine, self.up, h * 9 + 1)
+        self.c.start(mine, mine, self.down, h * 9 + 2)
 
     def relay(self, h):
         got = self.block(self.mirror, h)
-        self.c.arrived(got, h * 7, self.mirror)
-        for i, peer in enumerate(self.peers):
-            self.c.start(got, got, peer, h * 7 + 4 + i)
+        self.c.arrived(got, h * 9, self.mirror)
+        self.c.start(got, got, self.up, h * 9 + 3)
+        self.c.start(got, got, self.down, h * 9 + 4)
+
+    def forward(self, h):
+        for i in range(2):
+            self.c.arrived(self.block(self.downs[i], h), h * 9 + 1 + 2 * i, self.down)
+            part = self.block(self.downs[i], h, 0)
+            self.c.start(part, part, self.up, h * 9 + 5 + 2 * i)
+            self.c.arrived(self.block(self.ups[i], h), h * 9 + 2 + 2 * i, self.up)
+            part = self.block(self.ups[i], h, 1)
+            self.c.start(part, part, self.down, h * 9 + 6 + 2 * i)
 
     def rest(self, h):
-        for i, j in enumerate((1, 0, 2)):
-            self.c.arrived(self.block(self.peers[j], h), h * 7 + 1 + i, self.peers[j])
-            self.c.arrived(self.block(self.mirrors[j], h), h * 7 + 4 + i, self.peers[j])
+        for i in range(2):
+            self.c.arrived(self.block(self.fars[i], h, 0), h * 9 + 5 + 2 * i, self.down)
+            self.c.arrived(self.block(self.fars[i], h, 1), h * 9 + 6 + 2 * i, self.up)
 
 
 class Exchange:
@@ -291,7 +322,7 @@
     q_hbm, k_hbm, v_hbm, gain, routes, scores, cot_hbm, wg_hbm, wu_hbm, wd_hbm,
     mixed_out, gi_out, gg_out, gu_out, gd_out,
     xbuf, dybuf, wg, wu, wd, hid, dgb, dub, dhb, py, px,
-    core_in, far_in, near_in, across_in, gg, gu, gd,
+    core_in, far_in, near_in, across_in, far_across_in, gg, gu, gd,
     q, kv, attn, cot, slabs_out, slabs_in, spots_out, spots_in, place, mix_hi, mix_lo,
     send, recv, local_sem,
 ):
@@ -313,12 +344,12 @@
     def copies(tensor, axis="ctx"):
         return Copies(send, recv, tensor, axis)
 
-    gx = Gather(copies(0), xbuf, rows, width, p)
-    gy = Gather(copies(1), dybuf, rows, width, p)
+    gx = Gather(copies(0), xbuf, rows, width, p, True)
+    gy = Gather(copies(1), dybuf, rows, width, p, True)
     ry = Reduce(copies(2), py, core_in.at[0], far_in.at[0], near_in.at[0],
-                across_in.at[0], rows, width, p)
+                across_in.at[0], far_across_in.at[0], rows, width, p)
     rx = Reduce(copies(3), px, core_in.at[1], far_in.at[1], near_in.at[1],
-                across_in.at[1], rows, width, p)
+                across_in.at[1], far_across_in.at[1], rows, width, p)
     gk = Gather(copies(4), kv, tok, 2 * head, p)
     ga = HeadGather(copies(5, "exp"), attn, head, group, e)
     grads_there = Exchange(copies(6, "exp"), slabs_out.at[0], slabs_in.at[0], local_sem.at[8], e, n_exp)
@@ -417,9 +448,13 @@
         ga.own(h)
     for h in range(group):
         ga.relay(h)
+    gy.beside(0)
     gy.across()
     for h in range(group):
+        ga.forward(h)
+    for h in range(group):
         ga.rest(h)
+    gy.far(0)
 
     def squares(n, total):
         part = attn[:, pl.ds(pl.multiple_of(n * chunk, 128), chunk)].astype(f32)
@@ -465,13 +500,20 @@
             dub[pl.ds(at, col), cols] = (dh * silu).astype(bf16)
             dgb[pl.ds(at, col), cols] = (dh * u * sig * (1.0 + g * (1.0 - sig))).astype(bf16)
 
-    def second_half(x):
+    def expert_out(x):
         at = pl.multiple_of(x * col, 16)
 
         @pl.loop(0, width // wtile)
         def _(n):
             spot = pl.ds(pl.multiple_of(n * wtile, 128), wtile)
             py[pl.ds(at, col), spot] = dot(hid[pl.ds(at, col), :], wd[:, spot]).astype(bf16)
+
+    def input_grad(x):
+        at = pl.multiple_of(x * col, 16)
+
+        @pl.loop(0, width // wtile)
+        def _(n):
+            spot = pl.ds(pl.multiple_of(n * wtile, 128), wtile)
             px[pl.ds(at, col), spot] = (
                 dot(dgb[pl.ds(at, col), :], wg[spot, :], ((1,), (1,)))
                 + dot(dub[pl.ds(at, col), :], wu[spot, :], ((1,), (1,)))
@@ -489,11 +531,16 @@
             pltpu.make_async_copy(gg.at[spot, :], gg_out.at[spot, :], local_sem.at[6]).start()
             pltpu.make_async_copy(gu.at[spot, :], gu_out.at[spot, :], local_sem.at[7]).start()
 
-    def column(which, x):
-        first_half(x)
-        second_half(x)
+    def rest_of_column(which, x):
+        expert_out(x)
         ry.core_send(which)
+        input_grad(x)
         rx.core_send(which)
+
+    def near_early(which):
+        for work in (ry, rx):
+            work.core_add(which)
+            work.near_early(which - 1)
 
     def to_slabs(buf, which):
         row, to_row = iota((slots, rows), 1), iota((slots, rows), 0)
@@ -509,49 +556,60 @@
     def from_slabs(which, spot):
         return slabs_in[which, :, :, spot].astype(f32).reshape(slots, chunk).astype(bf16)
 
-    gy.beside(0)
     gy.beside(1)
     gy.other_core("own")
     back_half(p.x)
-    gy.far(0)
-    gx.across()
     gy.other_core("right")
     gy.other_core("left")
     back_half(p.xr)
     back_half(p.xl)
     gy.far(1)
     gx.beside(0)
+    gx.across()
     gx.other_core("own")
-    column(0, p.x)
+    first_half(p.x)
+    rest_of_column(0, p.x)
+    gx.far(0)
     gy.other_core("far")
     back_half(p.xf)
     gx.beside(1)
     gx.other_core("right")
-    column(1, p.xr)
-    gx.far(0)
+    first_half(p.xr)
+    rest_of_column(1, p.xr)
     gx.other_core("left")
-    column(2, p.xl)
+    first_half(p.xl)
+    near_early(1)
+    rest_of_column(2, p.xl)
     gx.far(1)
-    for which in (1, 2, 0):
-        ry.core_add(which)
-        rx.core_add(which)
     gx.other_core("far")
-    column(3, p.xf)
+    first_half(p.xf)
+    near_early(2)
+    rest_of_column(3, p.xf)
     ry.core_add(3)
+    ry.far_across()
+    rx.core_add(3)
+    rx.far_across()
+    ry.core_add(0)
+    rx.core_add(0)
+    weight_grads(0, 2)
     ry.far_send()
-    rx.core_add(3)
+    ry.near_add(0)
+    weight_grads(2, 3)
     rx.far_send()
-    weight_grads(0, 1)
+    rx.near_add(0)
+    weight_grads(3, 4)
     ry.near_send()
-    weight_grads(1, 3)
+    weight_grads(4, 5)
     rx.near_send()
-    weight_grads(3, width // wtile)
-    ry.near_add(0)
+    weight_grads(5, width // wtile)
     ry.near_add(1)
     ry.finish()
     to_slabs(py, 1)
     y_back.start()
-    rx.near_add(0)
+    rx.near_add(1)
+    rx.finish()
+    to_slabs(px, 2)
+    dx_back.start()
     y_back.finish()
 
     @pl.loop(0, width // chunk)
@@ -560,10 +618,6 @@
         slabs = from_slabs(1, spot)
         mixed_out[:, spot] = (dot(mix_hi[...], slabs) + dot(mix_lo[...], slabs)).astype(bf16)
 
-    rx.near_add(1)
-    rx.finish()
-    to_slabs(px, 2)
-    dx_back.start()
     dx_back.finish()
     mine = pl.ds(pl.multiple_of(e * tok_dev, 16), tok_dev)
     feats = attn[mine, :].astype(f32)
@@ -616,8 +670,9 @@
             pltpu.VMEM((total, width), bf16),
             pltpu.VMEM((total, width), bf16),
             pltpu.VMEM((2, 4, 2, rows, width), bf16),
-            pltpu.VMEM((2, 2, 2, rows, width // 2), bf16),
+            pltpu.VMEM((2, 2, rows, width // 2), bf16),
             pltpu.VMEM((2, 2, 2, rows, width), bf16),
+            pltpu.VMEM((2, rows, width), bf16),
             pltpu.VMEM((2, rows, width), bf16),
             pltpu.VMEM(gate_w.shape, bf16),
             pltpu.VMEM(up_w.shape, bf16),
@@ -633,8 +688,8 @@
             pltpu.VMEM((tok_dev, slots), bf16),
             pltpu.VMEM((tok_dev, slots), bf16),
             pltpu.VMEM((tok_dev, slots), bf16),
-            pltpu.SemaphoreType.DMA((10, 21)),
-            pltpu.SemaphoreType.DMA((10, 21)),
+            pltpu.SemaphoreType.DMA((10, 27)),
+            pltpu.SemaphoreType.DMA((10, 27)),
             pltpu.SemaphoreType.DMA((12,)),
         ],
         compiler_params=pltpu.CompilerParams(

time: 151 us -> 142 us (0.940)
  Pallas kernels: 133 us -> 125 us
    pallas_call x1, Pallas kernels: 133 us -> 125 us  [local(): pl.pallas_call(functools.partial(kernel, rows, width, hidden, head, group...]
where the time goes in v4:
time: 142 us; the launch traced here: 140 us
  Pallas kernels  125 us (88%)
  local copies, waits for them, and re-layouts  14.4 us (10%)
    pallas_call x1, Pallas kernels, local(): pl.pallas_call(functools.partial(kernel, rows, width, hidden, head, group...  125 us
    unnamed x11, local copies, waits for them, and re-layouts  14.4 us

profile of v4, /device:TPU:8, one launch (start us, length us, event | category | flops | bytes accessed | tf_op | source)
XLA Modules:
  0.0 139.9 jit_solution(7545340832501204515)
XLA Ops:
  0.6 1.4 copy.15.routes
  2.0 1.4 copy.16.scores
  3.3 124.9 %layer.1 = (bf16[16,3072]{1,0:T(8,128)(2,1)}, bf16[16,3072]{1,0:T(8,128)(2,1)}, bf16[3072,512]{1,0:T(8,128)(2,1)}, bf16[3072,512]{1,0:T(8,128)(2,1)}, bf16[512,3072]{1,0:T(8,128)(2,1)}) custom-call(bf16[128,384]{1,0:T(8,128)(2,1)} %q_hbm.1, bf16[128,128]{1,0:T(8,128)(2,1)} %k_hbm.1, bf16[128,128]{1,0:T(8,128)(2,1)} %v_hbm.1, f32[1,3072]{1,0:T(1,128)} %bitcast.13, ...), custom_call_target="tpu_custom_call" | custom-call | tf_op jit(solution)/shard_map/layer/pallas_call | solution.py:649
  128.2 1.5 %copy.22 = bf16[16,3072]{1,0:T(8,128)(2,1)} copy(bf16[16,3072]{1,0:T(8,128)(2,1)} %get-tuple-element.20) | data formatting | bytes 196608
  129.8 1.5 %copy.23 = bf16[16,3072]{1,0:T(8,128)(2,1)} copy(bf16[16,3072]{1,0:T(8,128)(2,1)} %get-tuple-element.21) | data formatting | bytes 196608
  131.3 0.0 copy-start.1
  131.3 3.9 %copy.24 = bf16[1,3072,512]{2,1,0:T(8,128)(2,1)} copy(bf16[1,3072,512]{2,1,0:T(8,128)(2,1)} %bitcast.12) | data formatting | bytes 6291456
  135.2 0.0 copy-done.1
  135.2 0.0 copy-start
  135.2 1.7 %copy.25 = bf16[1,3072,512]{2,1,0:T(8,128)(2,1)} copy(bf16[1,3072,512]{2,1,0:T(8,128)(2,1)S(1)} %bitcast.11) | data formatting | bytes 6291456
  136.9 1.4 copy-done
  138.2 1.7 %copy.26 = bf16[1,512,3072]{2,1,0:T(8,128)(2,1)} copy(bf16[1,512,3072]{2,1,0:T(8,128)(2,1)S(1)} %bitcast.10) | data formatting | bytes 6291456
Async XLA Ops:
  131.3 3.9 %copy-start.1 = (bf16[3072,512]{1,0:T(8,128)(2,1)S(1)}, bf16[3072,512]{1,0:T(8,128)(2,1)}, u32[]{:S(2)}) copy-start(bf16[3072,512]{1,0:T(8,128)(2,1)} %get-tuple-element.13) | copy-start | bytes 9437188
  135.2 3.0 %copy-start = (bf16[512,3072]{1,0:T(8,128)(2,1)S(1)}, bf16[512,3072]{1,0:T(8,128)(2,1)}, u32[]{:S(2)}) copy-start(bf16[512,3072]{1,0:T(8,128)(2,1)} %get-tuple-element.14) | copy-start | bytes 9437188

commit v5 on v4

--- a/solution.py
+++ b/solution.py
@@ -320,9 +320,9 @@
 def kernel(
     rows, width, hidden, head, group, n_exp,
     q_hbm, k_hbm, v_hbm, gain, routes, scores, cot_hbm, wg_hbm, wu_hbm, wd_hbm,
-    mixed_out, gi_out, gg_out, gu_out, gd_out,
+    mixed_out, gi_out, gg, gu, gd,
     xbuf, dybuf, wg, wu, wd, hid, dgb, dub, dhb, py, px,
-    core_in, far_in, near_in, across_in, far_across_in, gg, gu, gd,
+    core_in, far_in, near_in, across_in, far_across_in,
     q, kv, attn, cot, slabs_out, slabs_in, spots_out, spots_in, place, mix_hi, mix_lo,
     send, recv, local_sem,
 ):
@@ -527,9 +527,6 @@
             xt = xbuf[:, spot]
             gg[spot, :] = dot(xt, dgb[...], ((0,), (0,))).astype(bf16)
             gu[spot, :] = dot(xt, dub[...], ((0,), (0,))).astype(bf16)
-            pltpu.make_async_copy(gd.at[:, spot], gd_out.at[:, spot], local_sem.at[5]).start()
-            pltpu.make_async_copy(gg.at[spot, :], gg_out.at[spot, :], local_sem.at[6]).start()
-            pltpu.make_async_copy(gu.at[spot, :], gu_out.at[spot, :], local_sem.at[7]).start()
 
     def rest_of_column(which, x):
         expert_out(x)
@@ -626,11 +623,19 @@
     weighted = dot(place[...], back) * gain[...]
     inner = jnp.sum(weighted * feats, axis=1, keepdims=True) / width
     gi_out[...] = (inv_own * weighted - feats * (inv_own * inv_own * inv_own * inner)).astype(bf16)
-    pltpu.make_async_copy(gd, gd_out, local_sem.at[5]).wait()
-    pltpu.make_async_copy(gg, gg_out, local_sem.at[6]).wait()
-    pltpu.make_async_copy(gu, gu_out, local_sem.at[7]).wait()
     for work in (gx, gy, ry, rx, gk, ga, grads_there, spots_there, y_back, dx_back):
         work.c.drain()
+
+
+def put_out(*refs):
+    n = len(refs) // 2
+    copies = [
+        pltpu.make_async_copy(refs[i], refs[n + i], refs[-1].at[i]) for i in range(n)
+    ]
+    for copy in copies:
+        copy.start()
+    for copy in copies:
+        copy.wait()
 
 
 def local(queries, keys, values, norm_gain, routes, route_scores, cotangent, w_gate, w_up, w_down):
@@ -649,14 +654,14 @@
     mixed, grad_input, grad_gate, grad_upw, grad_down = pl.pallas_call(
         functools.partial(kernel, rows, width, hidden, head, group, n_exp),
         out_shape=(
-            jax.ShapeDtypeStruct((tok_dev, width), bf16),
-            jax.ShapeDtypeStruct((tok_dev, width), bf16),
-            jax.ShapeDtypeStruct(gate_w.shape, bf16),
-            jax.ShapeDtypeStruct(up_w.shape, bf16),
-            jax.ShapeDtypeStruct(down_w.shape, bf16),
+            pltpu.VMEM((tok_dev, width), bf16),
+            pltpu.VMEM((tok_dev, width), bf16),
+            pltpu.VMEM(gate_w.shape, bf16),
+            pltpu.VMEM(up_w.shape, bf16),
+            pltpu.VMEM(down_w.shape, bf16),
         ),
         in_specs=[hbm, hbm, hbm, vmem, vmem, vmem, hbm, hbm, hbm, hbm],
-        out_specs=[vmem, vmem, hbm, hbm, hbm],
+        out_specs=[vmem] * 5,
         scratch_shapes=[
             pltpu.VMEM((total, width), bf16),
             pltpu.VMEM((total, width), bf16),
@@ -674,9 +679,6 @@
             pltpu.VMEM((2, 2, 2, rows, width), bf16),
             pltpu.VMEM((2, rows, width), bf16),
             pltpu.VMEM((2, rows, width), bf16),
-            pltpu.VMEM(gate_w.shape, bf16),
-            pltpu.VMEM(up_w.shape, bf16),
-            pltpu.VMEM(down_w.shape, bf16),
             pltpu.VMEM(queries.shape, bf16),
             pltpu.VMEM((tok * NX * NY * NC, 2 * head), bf16),
             pltpu.VMEM((tok, width), bf16),
@@ -693,13 +695,23 @@
             pltpu.SemaphoreType.DMA((12,)),
         ],
         compiler_params=pltpu.CompilerParams(
-            collective_id=0, has_side_effects=True, vmem_limit_bytes=67000000
+            collective_id=0, has_side_effects=True, vmem_limit_bytes=54000000
         ),
         name="layer",
     )(
         queries, keys, values, norm_gain.reshape(1, width), routes, route_scores, cotangent,
         gate_w, up_w, down_w,
     )
+    results = (mixed, grad_input, grad_gate, grad_upw, grad_down)
+    mixed, grad_input, grad_gate, grad_upw, grad_down = pl.pallas_call(
+        put_out,
+        out_shape=tuple(jax.ShapeDtypeStruct(r.shape, r.dtype) for r in results),
+        in_specs=[hbm] * 5,
+        out_specs=[hbm] * 5,
+        scratch_shapes=[pltpu.SemaphoreType.DMA((5,))],
+        compiler_params=pltpu.CompilerParams(vmem_limit_bytes=1000000),
+        name="put_out",
+    )(*results)
     return (mixed, grad_input, grad_gate[None], grad_upw[None], grad_down[None])
 
 

time: 142 us -> 134 us (0.944)
  local copies, waits for them, and re-layouts: 14.4 us -> 2.71 us
  Pallas kernels: 125 us -> 128 us
    unnamed x11 -> x2, local copies, waits for them, and re-layouts: 14.4 us -> 2.71 us
    pallas_call x0 -> x1, Pallas kernels: none -> 3.85 us  [local(): pl.pallas_call(put_out, out_shape=tuple((jax.ShapeDtypeStruct(r.shape, r....]
where the time goes in v5:
time: 134 us; the launch traced here: 132 us
  Pallas kernels  128 us (96%)
  local copies, waits for them, and re-layouts  2.71 us (2%)
    pallas_call x1, Pallas kernels, local(): pl.pallas_call(functools.partial(kernel, rows, width, hidden, head, group...  124 us
    pallas_call x1, Pallas kernels, local(): pl.pallas_call(put_out, out_shape=tuple((jax.ShapeDtypeStruct(r.shape, r....  3.85 us
    unnamed x2, local copies, waits for them, and re-layouts  2.71 us

profile of v5, /device:TPU:8, one launch (start us, length us, event | category | flops | bytes accessed | tf_op | source)
XLA Modules:
  0.0 131.5 jit_solution(13956730284462445323)
XLA Ops:
  0.6 1.4 %copy.15.routes = s32[16,2]{1,0:T(8,128)} copy(s32[16,2]{0,1:T(2,128)} %param.14) | data formatting | bytes 256 | tf_op args[4]
  2.0 1.4 %copy.16.scores = f32[16,2]{1,0:T(8,128)} copy(f32[16,2]{0,1:T(2,128)} %param.15) | data formatting | bytes 256 | tf_op args[5]
  3.3 124.2 %layer.1 = (bf16[16,3072]{1,0:T(8,128)(2,1)S(1)}, bf16[16,3072]{1,0:T(8,128)(2,1)S(1)}, bf16[3072,512]{1,0:T(8,128)(2,1)S(1)}, bf16[3072,512]{1,0:T(8,128)(2,1)S(1)}, bf16[512,3072]{1,0:T(8,128)(2,1)S(1)}) custom-call(bf16[128,384]{1,0:T(8,128)(2,1)} %q_hbm.1, bf16[128,128]{1,0:T(8,128)(2,1)} %k_hbm.1, bf16[128,128]{1,0:T(8,128)(2,1)} %v_hbm.1, ...), custom_call_target="tpu_custom_call" | custom-call | tf_op jit(solution)/shard_map/layer/pallas_call | solution.py:654
  127.5 3.8 %put_out.1 = (bf16[16,3072]{1,0:T(8,128)(2,1)}, bf16[16,3072]{1,0:T(8,128)(2,1)}, bf16[3072,512]{1,0:T(8,128)(2,1)}, bf16[3072,512]{1,0:T(8,128)(2,1)}, bf16[512,3072]{1,0:T(8,128)(2,1)}) custom-call(bf16[16,3072]{1,0:T(8,128)(2,1)S(1)} %get-tuple-element.15.refs_0_, bf16[16,3072]{1,0:T(8,128)(2,1)S(1)} %get-tuple-element.16.refs_1_, ...), custom_call_target="tpu_custom_call" | custom-call | tf_op jit(solution)/shard_map/put_out/pallas_call | solution.py:706

commit v6 on v5

--- a/solution.py
+++ b/solution.py
@@ -143,7 +143,7 @@
 def add_into(dst, rows, count, width, first, sources):
     step = 768
 
-    @pl.loop(0, width // step)
+    @pl.loop(0, width // step, unroll=True)
     def _(i):
         at = pl.multiple_of(i * step, 128)
         spot = pl.multiple_of(first + i * step, 128)
@@ -402,7 +402,7 @@
     first[2].wait()
     chunk = 512
 
-    @pl.loop(0, width // chunk)
+    @pl.loop(0, width // chunk, unroll=True)
     def _(n):
         spot = pl.ds(pl.multiple_of(n * chunk, 128), chunk)
         part = dot(mix_hi[...], cot[:, spot], ((0,), (0,))) + dot(mix_lo[...], cot[:, spot], ((0,), (0,)))
@@ -422,7 +422,7 @@
     grads_there.finish()
     own_rows = pl.ds(pl.multiple_of(((p.x * NY + p.y) * NC + p.k) * rows, 16), rows)
 
-    @pl.loop(0, width // chunk)
+    @pl.loop(0, width // chunk, unroll=True)
     def _(n):
         spot = pl.ds(pl.multiple_of(n * chunk, 128), chunk)
         slabs = slabs_in[0, :, :, spot].astype(f32).reshape(slots, chunk).astype(bf16)
@@ -460,10 +460,10 @@
         part = attn[:, pl.ds(pl.multiple_of(n * chunk, 128), chunk)].astype(f32)
         return total + jnp.sum(part * part, axis=1, keepdims=True)
 
-    total = lax.fori_loop(0, width // chunk, squares, jnp.zeros((tok, 1), f32))
+    total = lax.fori_loop(0, width // chunk, squares, jnp.zeros((tok, 1), f32), unroll=True)
     inv = lax.rsqrt(total / width + norm_eps)
 
-    @pl.loop(0, width // chunk)
+    @pl.loop(0, width // chunk, unroll=True)
     def _(n):
         spot = pl.ds(pl.multiple_of(n * chunk, 128), chunk)
         normed = (attn[:, spot].astype(f32) * inv * gain[:, spot]).astype(bf16)
@@ -544,7 +544,7 @@
         source = (row * 43) >> 8
         spread = jnp.where(to_row == source * slot + (row - source * 6), 1.0, 0.0).astype(bf16)
 
-        @pl.loop(0, width // chunk)
+        @pl.loop(0, width // chunk, unroll=True)
         def _(n):
             spot = pl.ds(pl.multiple_of(n * chunk, 128), chunk)
             part = dot(spread, buf[own_rows, spot])
@@ -609,7 +609,7 @@
     dx_back.start()
     y_back.finish()
 
-    @pl.loop(0, width // chunk)
+    @pl.loop(0, width // chunk, unroll=True)
     def _(n):
         spot = pl.ds(pl.multiple_of(n * chunk, 128), chunk)
         slabs = from_slabs(1, spot)

time: 134 us -> 133 us (level)
  no operation moved by 1% of the time
where the time goes in v6:
time: 133 us; the launch traced here: 132 us
  Pallas kernels  128 us (96%)
  local copies, waits for them, and re-layouts  2.71 us (2%)
    pallas_call x1, Pallas kernels, local(): pl.pallas_call(functools.partial(kernel, rows, width, hidden, head, group...  124 us
    pallas_call x1, Pallas kernels, local(): pl.pallas_call(put_out, out_shape=tuple((jax.ShapeDtypeStruct(r.shape, r....  3.85 us
    unnamed x2, local copies, waits for them, and re-layouts  2.71 us

profile of v6, /device:TPU:8, one launch (start us, length us, event | category | flops | bytes accessed | tf_op | source)
XLA Modules:
  0.0 131.6 jit_solution(7195148369786582484)
XLA Ops:
  0.6 1.4 %copy.15.routes = s32[16,2]{1,0:T(8,128)} copy(s32[16,2]{0,1:T(2,128)} %param.14) | data formatting | bytes 256 | tf_op args[4]
  2.0 1.4 %copy.16.scores = f32[16,2]{1,0:T(8,128)} copy(f32[16,2]{0,1:T(2,128)} %param.15) | data formatting | bytes 256 | tf_op args[5]
  3.3 124.2 %layer.1 = (bf16[16,3072]{1,0:T(8,128)(2,1)S(1)}, bf16[16,3072]{1,0:T(8,128)(2,1)S(1)}, bf16[3072,512]{1,0:T(8,128)(2,1)S(1)}, bf16[3072,512]{1,0:T(8,128)(2,1)S(1)}, bf16[512,3072]{1,0:T(8,128)(2,1)S(1)}) custom-call(bf16[128,384]{1,0:T(8,128)(2,1)} %q_hbm.1, bf16[128,128]{1,0:T(8,128)(2,1)} %k_hbm.1, bf16[128,128]{1,0:T(8,128)(2,1)} %v_hbm.1, ...), custom_call_target="tpu_custom_call" | custom-call | tf_op jit(solution)/shard_map/layer/pallas_call | solution.py:654
  127.6 3.8 %put_out.1 = (bf16[16,3072]{1,0:T(8,128)(2,1)}, bf16[16,3072]{1,0:T(8,128)(2,1)}, bf16[3072,512]{1,0:T(8,128)(2,1)}, bf16[3072,512]{1,0:T(8,128)(2,1)}, bf16[512,3072]{1,0:T(8,128)(2,1)}) custom-call(bf16[16,3072]{1,0:T(8,128)(2,1)S(1)} %get-tuple-element.15.refs_0_, bf16[16,3072]{1,0:T(8,128)(2,1)S(1)} %get-tuple-element.16.refs_1_, ...), custom_call_target="tpu_custom_call" | custom-call | tf_op jit(solution)/shard_map/put_out/pallas_call | solution.py:706
